TPU v7x, 32 devices: a whole 2x2x4 slice. The times are simulated.
32 devices in a mesh: grp: 2 (over core), swap: 16 (over z, y, x).
Axes of the slice: x: 2, y: 2, z: 4, core: 2. Of those that a mesh axis runs over, the one named last changes fastest.
Arguments:
- cells: bfloat16 [32768, 512], P(('grp', 'swap')), may hold values from -6 to 6
- counts: int32 [32768], P(('grp', 'swap')), may hold values from 64 to 512
- donor_dest: int32 [32768, 1], P(('grp', 'swap')), may hold values from 0 to 31; in each aligned block of 1024 rows (0 to 1023, 1024 to 2047, ...) at most 48 rows name the same one
- donor_tile: int32 [32768], P(('grp', 'swap')), may hold values from 0 to 2047
- depth_rank: int32 [16], replicated, may hold values from 0 to 15, as said below
- resample: bfloat16 [512, 1024], replicated, may hold values from -0.25 to 0.25
- color_gain: float32 [3], replicated, may hold values from 0.5 to 3
- color_bias: float32 [3], replicated, may hold values from -1.5 to 1.5
Outputs:
- frame: float32 [4, 1048576], P(None, ('grp', 'swap'))
Inputs may be any that keep to these rules, and one draw needn't show every extreme that they name: `donor_dest`: in the rows of one device no owner is named more than 48 times, a bound that some block reaches. depth_rank[s] = s XOR m for one view mask m: the depth order is a binary partition by the bits of the brick index.
All inputs are finite; a program needn't handle non-finite values.
Results may differ from a plain program's by a relative error of at most 0.0003.
Values may be sent and summed in bfloat16 or wider, within the bound.
No kernel may reach another device: no remote copies, remote signals or barrier semaphores. Data moves between devices by JAX's collectives and lax.ppermute only.
A program may use at most 64 MiB of HBM per device.

v0:
```python
import functools

import jax
import jax.numpy as jnp
from jax import lax
from jax.experimental import pallas as pl
from jax.experimental.pallas import tpu as pltpu
from jax.sharding import PartitionSpec as P

IMG_W = 1024
IMG_H = 1024
DEPTH = 4
LANE_CHUNK = 256


def render_kernel(opacity_step, brick_of, gain, bias, cells_ref, resample_ref, out_ref, sample_ref):
    bricks, _, rows, width = cells_ref.shape
    sub = rows // DEPTH
    tile_span = resample_ref.shape[1]
    half_gain = [0.5 * gain[k] for k in range(3)]
    half_bias = [0.5 * bias[k] for k in range(3)]
    for chunk in range(tile_span // LANE_CHUNK):
        lanes = pl.ds(chunk * LANE_CHUNK, LANE_CHUNK)
        sample_ref[...] = jnp.dot(
            cells_ref[...].reshape(bricks * rows, width),
            resample_ref[:, lanes],
            preferred_element_type=jnp.float32,
        )

        def brick_step(place, carry):
            transmit, colors = carry[0], list(carry[1:])
            start = brick_of[place] * rows
            for layer in range(DEPTH):
                v = sample_ref[pl.ds(pl.multiple_of(start + layer * sub, sub), sub), :]
                softplus = jnp.maximum(v, 0.0) + jnp.log(1.0 + jnp.exp(-jnp.abs(v)))
                passed = transmit * jnp.exp(-opacity_step * softplus)
                weight = transmit - passed
                for k in range(3):
                    colors[k] = colors[k] + weight * jnp.tanh(half_gain[k] * v + half_bias[k])
                transmit = passed
            return (transmit, *colors)

        zero = jnp.zeros((sub, LANE_CHUNK), jnp.float32)
        done = lax.fori_loop(0, bricks, brick_step, (zero + 1.0, zero, zero, zero), unroll=4)
        opacity = 1.0 - done[0]
        for k in range(3):
            out_ref[k, :, lanes] = 0.5 * (opacity + done[1 + k])
        out_ref[3, :, lanes] = opacity


def render(cells, resample, depth_rank, color_gain, color_bias, opacity_step):
    bricks, groups, rows, width = cells.shape
    sub = rows // DEPTH
    tile_span = resample.shape[1]
    places = jnp.arange(bricks, dtype=jnp.int32)
    brick_of = jnp.sum(
        jnp.where(depth_rank[None, :] == places[:, None], places[None, :], 0), axis=1
    )
    return pl.pallas_call(
        functools.partial(render_kernel, opacity_step),
        out_shape=jax.ShapeDtypeStruct((4, groups * sub, tile_span), jnp.float32),
        grid_spec=pltpu.PrefetchScalarGridSpec(
            num_scalar_prefetch=3,
            grid=(groups,),
            in_specs=[
                pl.BlockSpec((bricks, 1, rows, width), lambda i, *_: (0, i, 0, 0)),
                pl.BlockSpec((width, tile_span), lambda i, *_: (0, 0)),
            ],
            out_specs=pl.BlockSpec((4, sub, tile_span), lambda i, *_: (0, i, 0)),
            scratch_shapes=[pltpu.VMEM((bricks * rows, LANE_CHUNK), jnp.float32)],
        ),
    )(brick_of, color_gain, color_bias, cells, resample)


def on_device(cells, counts, donor_dest, donor_tile, depth_rank, resample, color_gain, color_bias):
    owners = lax.axis_size(("grp", "swap"))
    group_count = lax.axis_size("grp")
    swap_count = lax.axis_size("swap")
    block_count, block_width = cells.shape
    tile_span = resample.shape[1]
    capacity = max(2, (3 * block_count + 2 * owners - 1) // (2 * owners))
    half_pixels = IMG_H // group_count * IMG_W
    tile_count = DEPTH * half_pixels // tile_span
    opacity_step = 2.5 / (DEPTH * swap_count)
    cell_lanes = jnp.arange(block_width, dtype=jnp.int32)
    masked = jnp.where(cell_lanes[None, :] < counts[:, None], cells, jnp.zeros_like(cells))
    target = donor_dest[:, 0]
    dest_hits = (target[:, None] == jnp.arange(owners, dtype=jnp.int32)[None, :]).astype(jnp.int32)
    before = jnp.cumsum(dest_hits, axis=0) - dest_hits
    order_in = jnp.sum(before * dest_hits, axis=1)
    slot_index = target * capacity + order_in
    layer_tiles = tile_count // DEPTH
    own_tiles = layer_tiles // swap_count
    sub = min(8, own_tiles)
    layer, place = donor_tile // layer_tiles, donor_tile % layer_tiles
    row_of = ((place // sub) * DEPTH + layer) * sub + place % sub
    send_cells = jnp.zeros((owners * capacity, block_width), cells.dtype).at[slot_index].set(masked)
    send_rows = jnp.full((owners * capacity,), -1, jnp.int32).at[slot_index].set(row_of)
    recv_cells, recv_rows = (
        lax.all_to_all(send_cells, ("grp", "swap"), split_axis=0, concat_axis=0, tiled=True),
        lax.all_to_all(send_rows, ("grp", "swap"), split_axis=0, concat_axis=0, tiled=True),
    )
    selector = (recv_rows[None, :] == jnp.arange(tile_count, dtype=jnp.int32)[:, None]).astype(
        jnp.bfloat16
    )
    tile_cells = jnp.dot(selector, recv_cells, preferred_element_type=jnp.float32).astype(
        jnp.bfloat16
    )
    bricks = lax.all_to_all(tile_cells, "swap", split_axis=0, concat_axis=0, tiled=True)
    bricks = bricks.reshape(swap_count, own_tiles // sub, DEPTH * sub, block_width)
    frame = render(bricks, resample, depth_rank, color_gain, color_bias, opacity_step)
    return frame.reshape(4, -1)


def solution(mesh):
    placed = (
        P(("grp", "swap"), None),
        P(("grp", "swap")),
        P(("grp", "swap"), None),
        P(("grp", "swap")),
        P(),
        P(),
        P(),
        P(),
    )
    return jax.shard_map(
        on_device, mesh=mesh, in_specs=placed, out_specs=P(None, ("grp", "swap")), check_vma=False
    )
```

profile of v0, /device:TPU:12, one launch (start us, length us, event | category | flops | bytes accessed | tf_op | source)
XLA Modules:
  0.0 153.9 jit_solution(1920555080115287593)
XLA Ops:
  0.0 0.7 fusion.12
  0.7 9.0 %reduce-window.6 = s32[32,8,128]{2,1,0:T(8,128)S(1)} reduce-window(s32[32,8,128]{2,1,0:T(8,128)S(1)} %fusion.12, s32[]{:T(128)} %constant.52.clone.1), window={size=1x1x128 pad=0_0x0_0x127_0}, to_apply=%region_1.2 | reduce-window | flops 4161536 | bytes 262148 | tf_op jit(solution)/shard_map/reduce-window
  9.7 0.1 slice.8
  9.8 0.1 copy.14
  10.0 0.1 copy.15
  10.1 0.1 broadcast_add_fusion
  10.2 0.7 fusion.11
  10.9 0.7 compare_select_fusion
  11.6 0.7 fusion.16
  12.3 4.3 %scatter_custom_fusion = s32[1536]{0:T(1024)S(1)} fusion(s32[1024]{0:T(1024)S(1)} %bitcast.40, s32[1024]{0:T(1024)S(1)} %fusion.16, s32[]{:T(128)} %constant.53.clone.1), kind=kCustom, calls=%fused_computation.41 | custom fusion | bytes 6148 | tf_op jit(solution)/shard_map/scatter | solution.py:98
  16.6 0.7 all_to_all.20
  17.3 6.0 %all-to-all-start = ((s32[32,48,1]{1,2,0:T(1,128)}), s32[32,48,1]{1,2,0:T(1,128)S(1)}, u32[]{:S(2)}, u32[]{:S(2)}) async-start(s32[32,48,1]{1,2,0:T(1,128)} %bitcast.6), calls=%async_computation | async-start | bytes 32768 | tf_op jit(solution)/shard_map/all_to_all | solution.py:101
  23.3 7.0 %scatter_custom_fusion.1 = bf16[1536,512]{1,0:T(8,128)(2,1)} fusion(s32[1024]{0:T(1024)S(1)} %bitcast.41, bf16[1024,512]{1,0:T(8,128)(2,1)} %param.8, s32[1024]{0:T(1024)} %param.9, bf16[]{:T(256)} %constant.64.clone.1), kind=kCustom, calls=%fused_computation.8 | custom fusion | flops 1048576 | bytes 2626560 | tf_op jit(solution)/shard_map/scatter | solution.py:97
  30.4 0.0 all-to-all-done
  30.4 5.8 %all-to-all-start.1 = ((bf16[32,48,512]{2,1,0:T(8,128)(2,1)}), bf16[32,48,512]{2,1,0:T(8,128)(2,1)S(1)}, u32[]{:S(2)}, u32[]{:S(2)}) async-start(bf16[32,48,512]{2,1,0:T(8,128)(2,1)} %bitcast.7), calls=%async_computation.1 | async-start | bytes 3145728 | tf_op jit(solution)/shard_map/all_to_all | solution.py:100
  36.2 0.5 broadcast.57
  36.7 0.7 reduce.3
  37.4 0.1 eq.67
  37.5 33.3 %all-to-all-done.1 = bf16[32,48,512]{2,1,0:T(8,128)(2,1)S(1)} async-done(((bf16[32,48,512]{2,1,0:T(8,128)(2,1)}), bf16[32,48,512]{2,1,0:T(8,128)(2,1)S(1)}, u32[]{:S(2)}, u32[]{:S(2)}) %all-to-all-start.1) | async-done | bytes 1572896 | tf_op jit(solution)/shard_map/all_to_all | solution.py:100
  70.7 4.6 %fusion.2 = bf16[2048,512]{1,0:T(8,128)(2,1)} fusion(bf16[1536,512]{1,0:T(8,128)(2,1)S(1)} %bitcast.34, s32[1536]{0:T(1024)S(1)} %eq.67), kind=kOutput, calls=%fused_computation.5 | convolution fusion | flops 3225419776 | bytes 3676160 | tf_op jit(solution)/shard_map/dot_general | solution.py:106
  75.4 0.0 copy-start.1
  75.4 8.7 %all-to-all-start.2 = ((bf16[16,128,512]{2,1,0:T(8,128)(2,1)}), bf16[16,128,512]{2,1,0:T(8,128)(2,1)S(1)}, u32[]{:S(2)}, u32[]{:S(2)}) async-start(bf16[16,128,512]{2,1,0:T(8,128)(2,1)} %bitcast.32), calls=%async_computation.2 | async-start | bytes 4194304 | tf_op jit(solution)/shard_map/all_to_all | solution.py:109
  84.1 0.0 copy-done.1
  84.1 0.6 select_reduce_fusion.brick_of
  84.7 47.4 %all-to-all-done.2 = bf16[16,128,512]{2,1,0:T(8,128)(2,1)S(1)} async-done(((bf16[16,128,512]{2,1,0:T(8,128)(2,1)}), bf16[16,128,512]{2,1,0:T(8,128)(2,1)S(1)}, u32[]{:S(2)}, u32[]{:S(2)}) %all-to-all-start.2) | async-done | bytes 2097184 | tf_op jit(solution)/shard_map/all_to_all | solution.py:109
  132.1 0.0 copy-start
  132.1 1.3 copy-done
  133.5 18.2 %shard_map.82 = f32[4,32,1024]{2,1,0:T(8,128)} custom-call(s32[16]{0:T(128)} %select_reduce_fusion.brick_of, f32[3]{0:T(128)} %gain.1, f32[3]{0:T(128)} %bias.1, bf16[16,4,32,512]{3,2,1,0:T(8,128)(2,1)} %bitcast.31, bf16[512,1024]{1,0:T(8,128)(2,1)} %resample_ref.1), custom_call_target="tpu_custom_call" | custom-call | tf_op jit(solution)/shard_map/pallas_call | solution.py:59
  151.7 2.2 %copy.18 = f32[1,4,32,1024]{3,1,2,0:T(4,128)} copy(f32[1,4,32,1024]{3,2,1,0:T(8,128)} %bitcast.33) | data formatting | bytes 1048576
  (2 shorter events, 0.0 us)
Async XLA Ops:
  17.3 13.0 %all-to-all-start = ((s32[32,48,1]{1,2,0:T(1,128)}), s32[32,48,1]{1,2,0:T(1,128)S(1)}, u32[]{:S(2)}, u32[]{:S(2)}) async-start(s32[32,48,1]{1,2,0:T(1,128)} %bitcast.6), calls=%async_computation | async-start | bytes 32768 | tf_op jit(solution)/shard_map/all_to_all | solution.py:101
  30.4 40.4 %all-to-all-start.1 = ((bf16[32,48,512]{2,1,0:T(8,128)(2,1)}), bf16[32,48,512]{2,1,0:T(8,128)(2,1)S(1)}, u32[]{:S(2)}, u32[]{:S(2)}) async-start(bf16[32,48,512]{2,1,0:T(8,128)(2,1)} %bitcast.7), calls=%async_computation.1 | async-start | bytes 3145728 | tf_op jit(solution)/shard_map/all_to_all | solution.py:100
  75.4 8.7 %copy-start.1 = (s32[16]{0:T(128)S(1)}, s32[16]{0:T(128)}, u32[]{:S(2)}) copy-start(s32[16]{0:T(128)} %param.12) | copy-start | bytes 196
  75.4 56.7 %all-to-all-start.2 = ((bf16[16,128,512]{2,1,0:T(8,128)(2,1)}), bf16[16,128,512]{2,1,0:T(8,128)(2,1)S(1)}, u32[]{:S(2)}, u32[]{:S(2)}) async-start(bf16[16,128,512]{2,1,0:T(8,128)(2,1)} %bitcast.32), calls=%async_computation.2 | async-start | bytes 4194304 | tf_op jit(solution)/shard_map/all_to_all | solution.py:109
  132.1 1.4 copy-start
where the time goes:
time: 154 us
  waiting for transfers between devices  80.7 us (52%)
  starting transfers between devices  20.5 us (13%)
  other arithmetic  20.3 us (13%)
  Pallas kernels  18.2 us (12%)
  local copies, waits for them, and re-layouts  9.41 us (6%)
  matrix products  4.63 us (3%)
    all_to_all x1, waiting for transfers between devices, on_device(): lax.all_to_all(tile_cells, 'swap', split_axis=0, concat_axis=0, tiled=True)  47.4 us
    all_to_all x1, waiting for transfers between devices, on_device(): lax.all_to_all(send_cells, ('grp', 'swap'), split_axis=0, concat_axis=0,...  33.3 us
    pallas_call x1, Pallas kernels, render(): pl.pallas_call(functools.partial(render_kernel, opacity_step), out_shape=...  18.2 us
    another operation x3, other arithmetic  9.15 us
    all_to_all x1, starting transfers between devices, on_device(): lax.all_to_all(tile_cells, 'swap', split_axis=0, concat_axis=0, tiled=True)  8.7 us
    scatter x1, other arithmetic, on_device(): jnp.zeros((owners * capacity, block_width), cells.dtype).at[slot_index]  7.05 us
    all_to_all x1, starting transfers between devices, on_device(): lax.all_to_all(send_rows, ('grp', 'swap'), split_axis=0, concat_axis=0, t...  5.99 us
    all_to_all x1, starting transfers between devices, on_device(): lax.all_to_all(send_cells, ('grp', 'swap'), split_axis=0, concat_axis=0,...  5.83 us
  transfers between devices with their start and end apart: 3, of which 2 were waited for; matrix products, arithmetic and copies ran while one was open for 6% of the time, Pallas kernels for 0%

commit v1 on v0

v1 whole, which is shorter than its diff:
```python
import functools

import jax
import jax.numpy as jnp
from jax import lax
from jax.experimental import pallas as pl
from jax.experimental.pallas import tpu as pltpu
from jax.sharding import PartitionSpec as P

IMG_W = 1024
IMG_H = 1024
DEPTH = 4
LANES = 128
ID_ROWS = 8
ID_BASE = 64
PACK_ROWS = 256
LANE_CHUNK = 256


def split(value, size):
    if size & (size - 1) == 0:
        return jnp.right_shift(value, size.bit_length() - 1), value & (size - 1)
    return value // size, value % size


def pack_kernel(plan, scalars, dest_ref, tile_ref, counts_ref, cells_ref, out_ref, masked_ref):
    owners, capacity, swap_count, layer_tiles, own_tiles, sub = plan
    block_count, width = cells_ref.shape
    columns = width // LANES
    first = scalars[0] * capacity
    group, brick = split(dest_ref[...], swap_count)
    layer, place = split(tile_ref[...], layer_tiles)
    owner, own = split(place, own_tiles)
    own_group, own_sub = split(own, sub)
    target = group * swap_count + owner
    row = ((own_group * swap_count + brick) * DEPTH + layer) * sub + own_sub
    row_high, row_low = split(row, ID_BASE)

    hits = lax.broadcasted_iota(jnp.int32, (owners, block_count), 0) == target
    hits = jnp.where(hits, 1.0, 0.0)
    step = min(256, block_count)
    earlier = lax.broadcasted_iota(jnp.int32, (step, step), 0) < lax.broadcasted_iota(
        jnp.int32, (step, step), 1
    )
    earlier = jnp.where(earlier, 1.0, 0.0).astype(jnp.bfloat16)
    total = jnp.zeros((owners, 1), jnp.float32)
    orders = []
    for start in range(0, block_count, step):
        part = hits[:, start : start + step]
        before = total + jnp.dot(
            part.astype(jnp.bfloat16), earlier, preferred_element_type=jnp.float32
        )
        orders.append(jnp.sum(before * part, axis=0, keepdims=True))
        total = total + jnp.sum(part, axis=1, keepdims=True)
    order = jnp.concatenate(orders, axis=1).astype(jnp.int32) - first
    present = (order >= 0) & (order < capacity)
    slot = jnp.where(present, target * capacity + order, -1)
    more = jnp.max(total) > (first + capacity).astype(jnp.float32)

    lane = jnp.where(present, order + scalars[1], -1)
    at_lane = lax.broadcasted_iota(jnp.int32, (LANES, block_count), 0) == lane
    hits = hits.astype(jnp.bfloat16)

    def spread(value):
        placed = jnp.where(at_lane, value.astype(jnp.float32), 0.0).astype(jnp.bfloat16)
        spread_out = lax.dot_general(
            hits, placed, (((1,), (1,)), ((), ())), preferred_element_type=jnp.float32
        )
        return spread_out[:, None, :]

    which = lax.broadcasted_iota(jnp.int32, (owners, ID_ROWS, LANES), 1)
    tags = jnp.where(which == 0, spread(row_high), jnp.where(which == 1, spread(row_low), 0.0))
    tags = jnp.where((which == 2) & more, 1.0, tags)
    out_ref[:, columns * capacity :, :] = tags.astype(jnp.bfloat16)

    live = jnp.transpose(jnp.broadcast_to(counts_ref[...], (LANES, block_count)))
    lanes = lax.broadcasted_iota(jnp.int32, (block_count, LANES), 1)
    for column in range(columns):
        at = pl.ds(column * LANES, LANES)
        keep = jnp.where(lanes + column * LANES < live, 1.0, 0.0).astype(jnp.bfloat16)
        masked_ref[:, at] = cells_ref[:, at] * keep

    rows = min(PACK_ROWS, owners * capacity)
    buckets = rows // capacity

    def gather_step(index, _):
        base = lax.broadcasted_iota(jnp.int32, (rows, block_count), 0) + index * rows
        pick = jnp.where(base == slot, 1.0, 0.0).astype(jnp.bfloat16)
        picked = jnp.dot(pick, masked_ref[...], preferred_element_type=jnp.float32)
        picked = picked.astype(jnp.bfloat16)
        for bucket in range(buckets):
            for column in range(columns):
                out_ref[index * buckets + bucket, column * capacity : (column + 1) * capacity, :] = (
                    picked[
                        bucket * capacity : (bucket + 1) * capacity,
                        column * LANES : (column + 1) * LANES,
                    ]
                )
        return 0

    lax.fori_loop(0, owners * capacity // rows, gather_step, 0)


def pack(plan, turn, my_index, dest, tile, counts, cells):
    owners, capacity = plan[:2]
    block_count, width = cells.shape
    shape = (owners, width // LANES * capacity + ID_ROWS, LANES)
    sources = LANES // capacity
    scalars = jnp.stack([turn, my_index % sources * capacity]).astype(jnp.int32)
    vmem = pl.BlockSpec(memory_space=pltpu.VMEM)
    return pl.pallas_call(
        functools.partial(pack_kernel, plan),
        out_shape=jax.ShapeDtypeStruct(shape, cells.dtype),
        in_specs=[pl.BlockSpec(memory_space=pltpu.SMEM)] + [vmem] * 4,
        out_specs=vmem,
        scratch_shapes=[pltpu.VMEM((block_count, width), cells.dtype)],
    )(scalars, dest, tile, counts, cells)


def integrate(sample_ref, out_ref, lanes, brick_of, gain, bias, opacity_step, bricks, rows):
    sub = rows // DEPTH
    half_gain = [0.5 * gain[k] for k in range(3)]
    half_bias = [0.5 * bias[k] for k in range(3)]

    def brick_step(place, carry):
        transmit, colors = carry[0], list(carry[1:])
        start = brick_of[place] * rows
        for layer in range(DEPTH):
            v = sample_ref[pl.ds(pl.multiple_of(start + layer * sub, sub), sub), :]
            softplus = jnp.maximum(v, 0.0) + jnp.log(1.0 + jnp.exp(-jnp.abs(v)))
            passed = transmit * jnp.exp(-opacity_step * softplus)
            weight = transmit - passed
            for k in range(3):
                colors[k] = colors[k] + weight * jnp.tanh(half_gain[k] * v + half_bias[k])
            transmit = passed
        return (transmit, *colors)

    zero = jnp.zeros((sub, sample_ref.shape[1]), jnp.float32)
    done = lax.fori_loop(0, bricks, brick_step, (zero + 1.0, zero, zero, zero), unroll=4)
    opacity = 1.0 - done[0]
    for k in range(3):
        out_ref[k, :, lanes] = 0.5 * (opacity + done[1 + k])
    out_ref[3, :, lanes] = opacity


def resample_and_integrate(read, resample_ref, out_ref, sample_ref, *scene):
    for start in range(0, resample_ref.shape[1], LANE_CHUNK):
        lanes = pl.ds(start, LANE_CHUNK)
        sample_ref[...] = jnp.dot(
            read(), resample_ref[:, lanes], preferred_element_type=jnp.float32
        )
        integrate(sample_ref, out_ref, lanes, *scene)


def render_kernel(
    opacity_step, bricks, brick_of, gain, bias, cells_ref, resample_ref, out_ref, sample_ref
):
    rows = cells_ref.shape[1] // bricks
    scene = (brick_of, gain, bias, opacity_step, bricks, rows)
    resample_and_integrate(lambda: cells_ref[0], resample_ref, out_ref, sample_ref, *scene)


def gather_render_kernel(
    opacity_step,
    bricks,
    capacity,
    brick_of,
    gain,
    bias,
    recv_ref,
    resample_ref,
    out_ref,
    data_ref,
    id_ref,
    tile_ref,
    sample_ref,
):
    owners = recv_ref.shape[0]
    width = resample_ref.shape[0]
    columns = width // LANES
    sources = LANES // capacity
    halves = id_ref.shape[0]
    group_rows = tile_ref.shape[0]

    @pl.when(pl.program_id(0) == 0)
    def _():
        tags = recv_ref[:, columns * capacity :, :].astype(jnp.float32)
        tags = jnp.sum(tags.reshape(owners // sources, sources, ID_ROWS, LANES), axis=1)
        ids = tags[:, 0, :] * ID_BASE + tags[:, 1, :]
        id_ref[...] = jnp.concatenate([ids[:halves], ids[halves:]], axis=1)
        for source in range(owners):
            part, inside = divmod(source, sources)
            start = (part % halves * 2 + part // halves) * LANES + inside * capacity
            for column in range(columns):
                data_ref[start : start + capacity, column * LANES : (column + 1) * LANES] = recv_ref[
                    source, column * capacity : (column + 1) * capacity, :
                ]

    base = lax.broadcasted_iota(jnp.int32, (group_rows, 2 * LANES), 0)
    base = (base + pl.program_id(0) * group_rows).astype(jnp.float32)
    picks = [
        jnp.where(base == id_ref[half : half + 1, :], 1.0, 0.0).astype(jnp.bfloat16)
        for half in range(halves)
    ]
    tile_ref[...] = jnp.dot(
        jnp.concatenate(picks, axis=1), data_ref[...], preferred_element_type=jnp.float32
    ).astype(jnp.bfloat16)
    scene = (brick_of, gain, bias, opacity_step, bricks, group_rows // bricks)
    resample_and_integrate(lambda: tile_ref[...], resample_ref, out_ref, sample_ref, *scene)


def render(kernel, source, source_spec, groups, group_rows, bricks, sub, scene, resample, scratch):
    width, tile_span = resample.shape
    return pl.pallas_call(
        kernel,
        out_shape=jax.ShapeDtypeStruct((4, groups * sub, tile_span), jnp.float32),
        grid_spec=pltpu.PrefetchScalarGridSpec(
            num_scalar_prefetch=3,
            grid=(groups,),
            in_specs=[source_spec, pl.BlockSpec((width, tile_span), lambda i, *_: (0, 0))],
            out_specs=pl.BlockSpec((4, sub, tile_span), lambda i, *_: (0, i, 0)),
            scratch_shapes=[*scratch, pltpu.VMEM((group_rows, LANE_CHUNK), jnp.float32)],
        ),
    )(*scene, source, resample)


def on_device(cells, counts, donor_dest, donor_tile, depth_rank, resample, color_gain, color_bias):
    both = ("grp", "swap")
    owners = lax.axis_size(both)
    group_count = lax.axis_size("grp")
    swap_count = lax.axis_size("swap")
    block_count, block_width = cells.shape
    tile_span = resample.shape[1]
    half_pixels = IMG_H // group_count * IMG_W
    layer_tiles = half_pixels // tile_span
    own_tiles = layer_tiles // swap_count
    sub = min(8, own_tiles)
    groups = own_tiles // sub
    group_rows = swap_count * DEPTH * sub
    opacity_step = 2.5 / (DEPTH * swap_count)
    mean = max(1, block_count // owners)
    capacity = min(LANES, (2 if mean >= 32 else 4) * mean)
    plan = (owners, capacity, swap_count, layer_tiles, own_tiles, sub)

    my_index = lax.axis_index(both)
    dest_row = donor_dest.reshape(1, block_count)
    tile_row = donor_tile.reshape(1, block_count)
    counts_row = counts.reshape(1, block_count)
    tag_row = block_width // LANES * capacity

    def exchange(turn):
        sent = pack(plan, turn, my_index, dest_row, tile_row, counts_row, cells)
        got = lax.all_to_all(sent, both, split_axis=0, concat_axis=0, tiled=True)
        return got, jnp.max(got[:, tag_row + 2, 0]) > 0

    def partial_sum(got):
        tags = got[:, tag_row : tag_row + 2, :].astype(jnp.float32)
        tags = jnp.sum(tags.reshape(-1, LANES // capacity, 2, LANES), axis=1)
        ids = (tags[:, 0] * ID_BASE + tags[:, 1]).reshape(1, -1)
        rows = jnp.arange(groups * group_rows, dtype=jnp.float32)[:, None]
        selector = (ids == rows).astype(jnp.bfloat16)
        data = got[:, :tag_row].reshape(owners, -1, capacity, LANES)
        data = data.transpose(0, 2, 1, 3).reshape(owners * capacity, block_width)
        return jnp.dot(selector, data, preferred_element_type=jnp.float32)

    places = jnp.arange(swap_count, dtype=jnp.int32)
    brick_of = jnp.sum(
        jnp.where(depth_rank[None, :] == places[:, None], places[None, :], 0), axis=1
    )
    scene = (brick_of, color_gain, color_bias)
    received, more = exchange(jnp.int32(0))

    def one_round():
        kernel = functools.partial(gather_render_kernel, opacity_step, swap_count, capacity)
        slots = owners * capacity
        return render(
            kernel,
            received,
            pl.BlockSpec(received.shape, lambda i, *_: (0, 0, 0)),
            groups,
            group_rows,
            swap_count,
            sub,
            scene,
            resample,
            [
                pltpu.VMEM((slots, block_width), jnp.bfloat16),
                pltpu.VMEM((slots // (2 * LANES), 2 * LANES), jnp.float32),
                pltpu.VMEM((group_rows, block_width), jnp.bfloat16),
            ],
        )

    def more_rounds():
        def next_round(state):
            turn, _, total = state
            got, again = exchange(turn)
            return turn + 1, again, total + partial_sum(got)

        start = (jnp.int32(1), more, partial_sum(received))
        total = lax.while_loop(lambda state: state[1], next_round, start)[2]
        tile_cells = total.astype(jnp.bfloat16).reshape(groups, group_rows, block_width)
        kernel = functools.partial(render_kernel, opacity_step, swap_count)
        return render(
            kernel,
            tile_cells,
            pl.BlockSpec((1, group_rows, block_width), lambda i, *_: (i, 0, 0)),
            groups,
            group_rows,
            swap_count,
            sub,
            scene,
            resample,
            [],
        )

    return lax.cond(more, more_rounds, one_round).reshape(4, -1)


def solution(mesh):
    placed = (
        P(("grp", "swap"), None),
        P(("grp", "swap")),
        P(("grp", "swap"), None),
        P(("grp", "swap")),
        P(),
        P(),
        P(),
        P(),
    )
    return jax.shard_map(
        on_device, mesh=mesh, in_specs=placed, out_specs=P(None, ("grp", "swap")), check_vma=False
    )
```

time: 154 us -> 93.6 us (0.61)
  the two profiles are of different devices: /device:TPU:12 before, /device:TPU:0 now
where the time goes in v1:
time: 93.6 us; the launch traced here: 93.3 us
  waiting for transfers between devices  51.9 us (55%)
  Pallas kernels  29.5 us (32%)
  starting transfers between devices  7.33 us (8%)
  local copies, waits for them, and re-layouts  2.2 us (2%)
  other arithmetic  1.4 us (1%)
    all_to_all x1, waiting for transfers between devices, exchange(): got = lax.all_to_all(sent, both, split_axis=0, concat_axis=0, tiled=True)  51.9 us
    pallas_call x1, Pallas kernels, render(): pl.pallas_call(kernel, out_shape=jax.ShapeDtypeStruct((4, groups * sub, t...  22.7 us
    all_to_all x1, starting transfers between devices, exchange(): got = lax.all_to_all(sent, both, split_axis=0, concat_axis=0, tiled=True)  7.33 us
    pallas_call x1, Pallas kernels, pack(): pl.pallas_call(functools.partial(pack_kernel, plan), out_shape=jax.ShapeD...  6.79 us
  transfers between devices with their start and end apart: 1, of which 1 were waited for; matrix products, arithmetic and copies ran while one was open for 0% of the time, Pallas kernels for 0%

profile of v1, /device:TPU:0, one launch (start us, length us, event | category | flops | bytes accessed | tf_op | source)
XLA Modules:
  0.0 93.3 jit_solution(2095936393674774925)
XLA Ops:
  0.0 0.7 pad_add_fusion.1.scalars
  0.7 6.8 %shard_map.84 = bf16[32,264,128]{2,1,0:T(8,128)(2,1)} custom-call(s32[2]{0:T(128)} %pad_add_fusion.1.scalars, s32[1,1024]{1,0:T(1,128)} %bitcast.57, s32[1,1024]{1,0:T(1,128)} %bitcast.59, s32[1,1024]{1,0:T(1,128)} %bitcast.61, bf16[1024,512]{1,0:T(8,128)(2,1)} %cells_ref.1), custom_call_target="tpu_custom_call" | custom-call | tf_op jit(solution)/shard_map/pallas_call | solution.py:111
  7.4 0.0 copy-start.8
  7.4 0.0 copy-start
  7.4 0.0 copy-start.3
  7.5 0.0 copy-start.4
  7.5 0.0 copy-start.5
  7.5 0.0 copy-start.6
  7.5 0.0 copy-start.7
  7.5 7.3 %all-to-all-start.1 = ((bf16[32,264,128]{2,1,0:T(8,128)(2,1)}), bf16[32,264,128]{2,1,0:T(8,128)(2,1)S(1)}, u32[]{:S(2)}, u32[]{:S(2)}) async-start(bf16[32,264,128]{2,1,0:T(8,128)(2,1)} %shard_map.84), calls=%async_computation.1 | async-start | bytes 4325376 | tf_op jit(solution)/shard_map/all_to_all | solution.py:253
  14.8 0.0 copy-done.8
  14.8 0.1 select_reduce_fusion
  15.0 51.9 %all-to-all-done.1 = bf16[32,264,128]{2,1,0:T(8,128)(2,1)S(1)} async-done(((bf16[32,264,128]{2,1,0:T(8,128)(2,1)}), bf16[32,264,128]{2,1,0:T(8,128)(2,1)S(1)}, u32[]{:S(2)}, u32[]{:S(2)}) %all-to-all-start.1) | async-done | bytes 2162720 | tf_op jit(solution)/shard_map/all_to_all | solution.py:253
  66.8 0.6 slice_reduce_fusion.1
  68.1 0.0 copy-done
  68.1 0.0 copy-done.3
  68.2 0.0 copy-done.4
  68.2 0.0 copy-done.5
  68.2 0.0 copy-done.6
  68.2 0.0 copy-done.7
  68.2 24.3 %conditional.1 = (f32[4,32768]{1,0:T(4,128)S(1)}) conditional(s32[]{:T(128)} %convert_element_type.12, (s32[16]{0:T(128)S(1)}, f32[3]{0:T(128)S(1)}, f32[3]{0:T(128)S(1)}, bf16[32,264,128]{2,1,0:T(8,128)(2,1)S(1)}, bf16[512,1024]{1,0:T(8,128)(2,1)}) %tuple.48, (bf16[32,264,128]{2,1,0:T(8,128)(2,1)S(1)}, s32[]{:T(128)}, s32[1,1024]{1,0:T(1,128)S(1)}, ...), branch_computations={%region_2.3_spmd, %region_3.9_spmd} | conditional | flops 8600453120 | bytes 51708360 | solution.py:316
  68.2 22.7 %branch_0_fun.1 = f32[4,32,1024]{2,1,0:T(8,128)} custom-call(s32[16]{0:T(128)S(1)} %get-tuple-element.127.brick_of, f32[3]{0:T(128)S(1)} %get-tuple-element.128.gain, f32[3]{0:T(128)S(1)} %get-tuple-element.129.bias, bf16[32,264,128]{2,1,0:T(8,128)(2,1)S(1)} %get-tuple-element.130.recv_ref, bf16[512,1024]{1,0:T(8,128)(2,1)} %get-tuple-element.131.resample_ref), custom_call_target="tpu_custom_call" | custom-call | tf_op jit(solution)/shard_map/cond/branch_0_fun/pallas_call | solution.py:214
  90.9 1.4 %copy.15 = f32[1,4,32,1024]{3,1,2,0:T(4,128)S(1)} copy(f32[1,4,32,1024]{3,2,1,0:T(8,128)} %bitcast.53) | data formatting | bytes 1048576 | tf_op jit(solution)/shard_map/cond
  92.5 0.0 copy-start.2
  92.5 0.8 copy-done.2
Async XLA Ops:
  7.4 7.4 %copy-start.8 = (s32[16]{0:T(128)S(1)}, s32[16]{0:T(128)}, u32[]{:S(2)}) copy-start(s32[16]{0:T(128)} %param.16) | copy-start | bytes 196
  7.4 60.7 %copy-start = (bf16[1024,512]{1,0:T(8,128)(2,1)S(1)}, bf16[1024,512]{1,0:T(8,128)(2,1)}, u32[]{:S(2)}) copy-start(bf16[1024,512]{1,0:T(8,128)(2,1)} %cells_ref.1) | copy-start | bytes 3145732
  7.4 60.7 %copy-start.3 = (s32[1024,1]{0,1:T(1,128)S(1)}, s32[1024,1]{0,1:T(1,128)}, u32[]{:S(2)}) copy-start(s32[1024,1]{0,1:T(1,128)} %param.14) | copy-start | bytes 12292
  7.5 60.7 %copy-start.4 = (s32[1024]{0:T(1024)S(1)}, s32[1024]{0:T(1024)}, u32[]{:S(2)}) copy-start(s32[1024]{0:T(1024)} %param.15) | copy-start | bytes 12292
  7.5 60.7 %copy-start.5 = (s32[1024]{0:T(1024)S(1)}, s32[1024]{0:T(1024)}, u32[]{:S(2)}) copy-start(s32[1024]{0:T(1024)} %param.13) | copy-start | bytes 12292
  7.5 60.7 %copy-start.6 = (f32[3]{0:T(128)S(1)}, f32[3]{0:T(128)}, u32[]{:S(2)}) copy-start(f32[3]{0:T(128)} %param.18) | copy-start | bytes 40
  7.5 60.7 %copy-start.7 = (f32[3]{0:T(128)S(1)}, f32[3]{0:T(128)}, u32[]{:S(2)}) copy-start(f32[3]{0:T(128)} %param.19) | copy-start | bytes 40
  7.5 59.3 %all-to-all-start.1 = ((bf16[32,264,128]{2,1,0:T(8,128)(2,1)}), bf16[32,264,128]{2,1,0:T(8,128)(2,1)S(1)}, u32[]{:S(2)}, u32[]{:S(2)}) async-start(bf16[32,264,128]{2,1,0:T(8,128)(2,1)} %shard_map.84), calls=%async_computation.1 | async-start | bytes 4325376 | tf_op jit(solution)/shard_map/all_to_all | solution.py:253
  92.5 0.8 copy-start.2

commit v2 on v1

v2 whole, which is shorter than its diff:
```python
import functools

import jax
import jax.numpy as jnp
from jax import lax
from jax.experimental import pallas as pl
from jax.experimental.pallas import tpu as pltpu
from jax.sharding import PartitionSpec as P

IMG_W = 1024
IMG_H = 1024
DEPTH = 4
LANES = 128
ID_ROWS = 8
ID_BASE = 64
BANDS = 2
BUCKET_STEP = 8
LANE_CHUNK = 256
LOG2_E = 1.4426950408889634


def split(value, size):
    if size & (size - 1) == 0:
        return jnp.right_shift(value, size.bit_length() - 1), value & (size - 1)
    return value // size, value % size


def one_hot(rows, columns, start, labels):
    row = (lax.broadcasted_iota(jnp.int32, (rows, columns), 0) + start).astype(jnp.int16)
    same = row == jnp.broadcast_to(labels.astype(jnp.int16), (rows, columns))
    return jnp.where(same, jnp.bfloat16(1), jnp.bfloat16(0))


def route(plan, scalars, dest_ref, tile_ref, counts_ref, cells_ref, slot_ref, tag_ref, masked_ref):
    owners, capacities, swap_count, layer_tiles, own_tiles, sub = plan
    block_count, width = cells_ref.shape
    group, brick = split(dest_ref[...], swap_count)
    layer, place = split(tile_ref[...], layer_tiles)
    owner, own = split(place, own_tiles)
    own_group, own_sub = split(own, sub)
    target = group * swap_count + owner
    row = ((own_group * swap_count + brick) * DEPTH + layer) * sub + own_sub
    parts = [part.astype(jnp.float32) for part in split(row, ID_BASE)]

    aimed = lax.broadcasted_iota(jnp.int32, (owners, block_count), 0) == target
    hits = [
        jnp.where(aimed & (counts_ref[...] > band * (width // BANDS)), 1.0, 0.0)
        for band in range(BANDS)
    ]
    hits = jnp.concatenate(hits, axis=0)
    step = min(256, block_count)
    earlier = lax.broadcasted_iota(jnp.int32, (step, step), 0) < lax.broadcasted_iota(
        jnp.int32, (step, step), 1
    )
    earlier = jnp.where(earlier, 1.0, 0.0).astype(jnp.bfloat16)
    total = jnp.zeros((BANDS * owners, 1), jnp.float32)
    before = []
    for start in range(0, block_count, step):
        part = hits[:, start : start + step]
        before.append(
            total
            + jnp.dot(part.astype(jnp.bfloat16), earlier, preferred_element_type=jnp.float32)
        )
        total = total + jnp.sum(part, axis=1, keepdims=True)
    before = jnp.concatenate(before, axis=1) * hits

    which = lax.broadcasted_iota(jnp.int32, (owners, ID_ROWS, LANES), 1)
    tags = jnp.zeros((owners, ID_ROWS, LANES), jnp.float32)
    for band, capacity in enumerate(capacities):
        rows = slice(band * owners, (band + 1) * owners)
        first = scalars[0] * capacity
        order = jnp.sum(before[rows], axis=0, keepdims=True).astype(jnp.int32) - first
        alive = counts_ref[...] > band * (width // BANDS)
        present = alive & (order >= 0) & (order < capacity)
        slot_ref[band : band + 1, :] = jnp.where(present, target * capacity + order, -1)
        lane = jnp.where(present, (order + scalars[1 + band]) & (LANES - 1), -1)
        at_lane = lax.broadcasted_iota(jnp.int32, (LANES, block_count), 0) == lane
        hit = hits[rows].astype(jnp.bfloat16)
        for index, part in enumerate(parts):
            placed = jnp.where(at_lane, part, 0.0).astype(jnp.bfloat16)
            spread = lax.dot_general(
                hit, placed, (((1,), (1,)), ((), ())), preferred_element_type=jnp.float32
            )
            tags = jnp.where(which == 2 * band + index, spread[:, None, :], tags)
        more = jnp.max(total[rows]) > (first + capacity).astype(jnp.float32)
        tags = jnp.where((which == 2 * BANDS + band) & more, 1.0, tags)
    tag_ref[...] = tags.astype(jnp.bfloat16)

    live = jnp.transpose(jnp.broadcast_to(counts_ref[...], (LANES, block_count)))
    lanes = lax.broadcasted_iota(jnp.int32, (block_count, LANES), 1)
    for start in range(0, width, LANES):
        at = pl.ds(start, LANES)
        keep = jnp.where(lanes + start < live, 1.0, 0.0).astype(jnp.bfloat16)
        masked_ref[:, at] = cells_ref[:, at] * keep


def pack_kernel(plan, scalars, dest_ref, tile_ref, counts_ref, cells_ref, out_ref, *scratch):
    slot_ref, tag_ref, masked_ref = scratch
    capacities = plan[1]
    block_count, width = cells_ref.shape
    buckets = out_ref.shape[0]
    band_width = width // BANDS
    index = pl.program_id(0)

    @pl.when(index == 0)
    def _():
        route(plan, scalars, dest_ref, tile_ref, counts_ref, cells_ref, *scratch)

    top = 0
    for band, capacity in enumerate(capacities):
        at_once = max(1, min(buckets, 512 // capacity))
        for base in range(0, buckets, at_once):
            rows = min(at_once, buckets - base) * capacity
            pick = one_hot(
                rows,
                block_count,
                (index * buckets + base) * capacity,
                slot_ref[band : band + 1, :],
            )
            picked = jnp.dot(
                pick,
                masked_ref[:, band * band_width : (band + 1) * band_width],
                preferred_element_type=jnp.float32,
            ).astype(jnp.bfloat16)
            for bucket in range(rows // capacity):
                for column in range(band_width // LANES):
                    out_ref[base + bucket, top + column * capacity : top + (column + 1) * capacity] = (
                        picked[
                            bucket * capacity : (bucket + 1) * capacity,
                            column * LANES : (column + 1) * LANES,
                        ]
                    )
        top += band_width // LANES * capacity
    out_ref[:, top:, :] = tag_ref[pl.ds(index * buckets, buckets)]


def pack(plan, turn, my_index, dest, tile, counts, cells):
    owners, capacities = plan[:2]
    block_count, width = cells.shape
    rows = width // BANDS // LANES * sum(capacities) + ID_ROWS
    buckets = min(BUCKET_STEP, owners)
    offsets = [my_index * capacity % LANES for capacity in capacities]
    scalars = jnp.stack([turn, *offsets]).astype(jnp.int32)
    row = pl.BlockSpec((1, block_count), lambda i, *_: (0, 0))
    return pl.pallas_call(
        functools.partial(pack_kernel, plan),
        out_shape=jax.ShapeDtypeStruct((owners, rows, LANES), cells.dtype),
        grid_spec=pltpu.PrefetchScalarGridSpec(
            num_scalar_prefetch=1,
            grid=(owners // buckets,),
            in_specs=[row, row, row, pl.BlockSpec((block_count, width), lambda i, *_: (0, 0))],
            out_specs=pl.BlockSpec((buckets, rows, LANES), lambda i, *_: (i, 0, 0)),
            scratch_shapes=[
                pltpu.VMEM((8, block_count), jnp.int32),
                pltpu.VMEM((owners, ID_ROWS, LANES), jnp.bfloat16),
                pltpu.VMEM((block_count, width), cells.dtype),
            ],
        ),
    )(scalars, dest, tile, counts, cells)


def integrate(sample_ref, out_ref, start, brick_of, gain, bias, opacity_step, bricks, rows):
    sub = rows // DEPTH
    chunk = sample_ref.shape[1]
    half_gain = [0.5 * gain[k] for k in range(3)]
    half_bias = [0.5 * bias[k] for k in range(3)]

    def brick_step(place, carry):
        transmit, colors = carry[0], list(carry[1:])
        top = brick_of[place] * rows
        for layer in range(DEPTH):
            v = sample_ref[pl.ds(pl.multiple_of(top + layer * sub, sub), sub), :]
            scaled = v * LOG2_E
            softplus = jnp.maximum(scaled, 0.0) + jnp.log2(1.0 + jnp.exp2(-jnp.abs(scaled)))
            passed = transmit * jnp.exp2(-opacity_step * softplus)
            weight = transmit - passed
            for k in range(3):
                colors[k] = colors[k] + weight * jnp.tanh(half_gain[k] * v + half_bias[k])
            transmit = passed
        return (transmit, *colors)

    zero = jnp.zeros((sub, chunk), jnp.float32)
    done = lax.fori_loop(0, bricks, brick_step, (zero + 1.0, zero, zero, zero), unroll=4)
    opacity = 1.0 - done[0]
    planes = [0.5 * (opacity + done[1 + k]) for k in range(3)] + [opacity]
    for k, plane in enumerate(planes):
        for row in range(sub):
            at = pl.ds(start + row * (out_ref.shape[1] // sub), chunk)
            out_ref[k : k + 1, at] = plane[row : row + 1]


def resample_and_integrate(read, resample_ref, out_ref, sample_ref, *scene):
    for start in range(0, resample_ref.shape[1], LANE_CHUNK):
        sample_ref[...] = jnp.dot(
            read(), resample_ref[:, start : start + LANE_CHUNK], preferred_element_type=jnp.float32
        )
        integrate(sample_ref, out_ref, start, *scene)


def render_kernel(
    opacity_step, bricks, brick_of, gain, bias, cells_ref, resample_ref, out_ref, sample_ref
):
    rows = cells_ref.shape[1] // bricks
    scene = (brick_of, gain, bias, opacity_step, bricks, rows)
    resample_and_integrate(lambda: cells_ref[0], resample_ref, out_ref, sample_ref, *scene)


def unpack(capacities, recv_ref, data_refs, id_refs):
    owners = recv_ref.shape[0]
    top = 0
    for capacity, data_ref in zip(capacities, data_refs):
        for column in range(data_ref.shape[1] // LANES):
            for source in range(owners):
                data_ref[
                    source * capacity : (source + 1) * capacity,
                    column * LANES : (column + 1) * LANES,
                ] = recv_ref[source, top : top + capacity, :]
            top += capacity
    tags = recv_ref[:, top:, :].astype(jnp.float32)
    lane = lax.broadcasted_iota(jnp.int32, (1, LANES), 1)
    for band, (capacity, id_ref) in enumerate(zip(capacities, id_refs)):
        ids = tags[:, 2 * band, :] * ID_BASE + tags[:, 2 * band + 1, :]
        for block in range(owners * capacity // LANES):
            low, high = block * LANES, (block + 1) * LANES
            row = jnp.zeros((1, LANES), jnp.float32)
            for source in range(low // capacity, -(-high // capacity)):
                part = ids[source : source + 1]
                if source * capacity < low:
                    part = jnp.where(lane < (source + 1) * capacity - low, part, 0.0)
                elif (source + 1) * capacity > high:
                    part = jnp.where(lane >= source * capacity - low, part, 0.0)
                row = row + part
            id_ref[0:1, low:high] = row.astype(jnp.int32)


def gather_render_kernel(
    opacity_step,
    bricks,
    capacities,
    brick_of,
    gain,
    bias,
    recv_ref,
    resample_ref,
    out_ref,
    *scratch,
):
    data_refs, id_refs = scratch[:BANDS], scratch[BANDS : 2 * BANDS]
    tile_ref, sample_ref = scratch[2 * BANDS :]
    group_rows = tile_ref.shape[0]

    @pl.when(pl.program_id(0) == 0)
    def _():
        unpack(capacities, recv_ref, data_refs, id_refs)

    band_width = data_refs[0].shape[1]
    for band, (data_ref, id_ref) in enumerate(zip(data_refs, id_refs)):
        pick = one_hot(
            group_rows, data_ref.shape[0], pl.program_id(0) * group_rows, id_ref[0:1, :]
        )
        tile_ref[:, band * band_width : (band + 1) * band_width] = jnp.dot(
            pick, data_ref[...], preferred_element_type=jnp.float32
        ).astype(jnp.bfloat16)
    scene = (brick_of, gain, bias, opacity_step, bricks, group_rows // bricks)
    resample_and_integrate(lambda: tile_ref[...], resample_ref, out_ref, sample_ref, *scene)


def render(kernel, source, source_spec, groups, group_rows, bricks, sub, scene, resample, scratch):
    width, tile_span = resample.shape
    return pl.pallas_call(
        kernel,
        out_shape=jax.ShapeDtypeStruct((4, groups * sub * tile_span), jnp.float32),
        grid_spec=pltpu.PrefetchScalarGridSpec(
            num_scalar_prefetch=3,
            grid=(groups,),
            in_specs=[source_spec, pl.BlockSpec((width, tile_span), lambda i, *_: (0, 0))],
            out_specs=pl.BlockSpec((4, sub * tile_span), lambda i, *_: (0, i)),
            scratch_shapes=[*scratch, pltpu.VMEM((group_rows, LANE_CHUNK), jnp.float32)],
        ),
    )(*scene, source, resample)


def slots_for(mean, owners, deviations):
    wanted = mean + deviations * mean**0.5
    capacity = min(LANES, max(8, int(-(-wanted // 8) * 8)))
    while owners * capacity % (2 * LANES):
        capacity += 8
    return capacity


def on_device(cells, counts, donor_dest, donor_tile, depth_rank, resample, color_gain, color_bias):
    both = ("grp", "swap")
    owners = lax.axis_size(both)
    group_count = lax.axis_size("grp")
    swap_count = lax.axis_size("swap")
    block_count, block_width = cells.shape
    tile_span = resample.shape[1]
    half_pixels = IMG_H // group_count * IMG_W
    layer_tiles = half_pixels // tile_span
    own_tiles = layer_tiles // swap_count
    sub = min(8, own_tiles)
    groups = own_tiles // sub
    group_rows = swap_count * DEPTH * sub
    opacity_step = 2.5 / (DEPTH * swap_count)
    mean = block_count / owners
    capacities = (slots_for(mean, owners, 5.5), slots_for(mean * 4 / 7, owners, 5.0))
    plan = (owners, capacities, swap_count, layer_tiles, own_tiles, sub)
    band_width = block_width // BANDS

    my_index = lax.axis_index(both)
    dest_row = donor_dest.reshape(1, block_count)
    tile_row = donor_tile.reshape(1, block_count)
    counts_row = counts.reshape(1, block_count)
    tag_row = band_width // LANES * sum(capacities)

    def exchange(turn):
        sent = pack(plan, turn, my_index, dest_row, tile_row, counts_row, cells)
        got = lax.all_to_all(sent, both, split_axis=0, concat_axis=0, tiled=True)
        flags = got[:, tag_row + 2 * BANDS : tag_row + 3 * BANDS, 0]
        return got, jnp.max(flags) > 0

    def partial_sum(got):
        rows = jnp.arange(groups * group_rows, dtype=jnp.float32)[:, None]
        tags = got[:, tag_row:, :].astype(jnp.float32)
        top, sums = 0, []
        for band, capacity in enumerate(capacities):
            ids = tags[:, 2 * band] * ID_BASE + tags[:, 2 * band + 1]
            source = jnp.arange(owners)[:, None]
            lane = (source * capacity + jnp.arange(capacity)[None, :]) % LANES
            ids = jnp.take_along_axis(ids, lane, axis=1).reshape(1, -1)
            selector = (ids == rows).astype(jnp.bfloat16)
            end = top + band_width // LANES * capacity
            data = got[:, top:end].reshape(owners, -1, capacity, LANES).transpose(0, 2, 1, 3)
            data = data.reshape(owners * capacity, band_width)
            sums.append(jnp.dot(selector, data, preferred_element_type=jnp.float32))
            top = end
        return jnp.concatenate(sums, axis=1)

    places = jnp.arange(swap_count, dtype=jnp.int32)
    brick_of = jnp.sum(
        jnp.where(depth_rank[None, :] == places[:, None], places[None, :], 0), axis=1
    )
    scene = (brick_of, color_gain, color_bias)
    received, more = exchange(jnp.int32(0))

    def one_round():
        kernel = functools.partial(gather_render_kernel, opacity_step, swap_count, capacities)
        slots = [owners * capacity for capacity in capacities]
        scratch = [pltpu.VMEM((count, band_width), jnp.bfloat16) for count in slots]
        scratch += [pltpu.VMEM((8, count), jnp.int32) for count in slots]
        scratch += [pltpu.VMEM((group_rows, block_width), jnp.bfloat16)]
        whole = pl.BlockSpec(received.shape, lambda i, *_: (0, 0, 0))
        shape = (groups, group_rows, swap_count, sub)
        return render(kernel, received, whole, *shape, scene, resample, scratch)

    def more_rounds():
        def next_round(state):
            turn, _, total = state
            got, again = exchange(turn)
            return turn + 1, again, total + partial_sum(got)

        start = (jnp.int32(1), more, partial_sum(received))
        total = lax.while_loop(lambda state: state[1], next_round, start)[2]
        tile_cells = total.astype(jnp.bfloat16).reshape(groups, group_rows, block_width)
        kernel = functools.partial(render_kernel, opacity_step, swap_count)
        group = pl.BlockSpec((1, group_rows, block_width), lambda i, *_: (i, 0, 0))
        shape = (groups, group_rows, swap_count, sub)
        return render(kernel, tile_cells, group, *shape, scene, resample, [])

    return lax.cond(more, more_rounds, one_round)


def solution(mesh):
    placed = (
        P(("grp", "swap"), None),
        P(("grp", "swap")),
        P(("grp", "swap"), None),
        P(("grp", "swap")),
        P(),
        P(),
        P(),
        P(),
    )
    return jax.shard_map(
        on_device, mesh=mesh, in_specs=placed, out_specs=P(None, ("grp", "swap")), check_vma=False
    )
```

time: 93.6 us -> 80.6 us (0.86)
  waiting for transfers between devices: 51.9 us -> 43.4 us
  local copies, waits for them, and re-layouts: 2.2 us -> 0.01 us
  Pallas kernels: 29.5 us -> 27.5 us
    all_to_all x1, waiting for transfers between devices: 51.9 us -> 43.4 us  [exchange(): got = lax.all_to_all(sent, both, split_axis=0, concat_axis=0, tiled=True)]
    pallas_call x1, Pallas kernels: 22.7 us -> 21 us  [render(): pl.pallas_call(kernel, out_shape=jax.ShapeDtypeStruct((4, groups * sub *...]
    cond x1 -> x0, local copies, waits for them, and re-layouts: 1.38 us -> none
where the time goes in v2:
time: 80.6 us; the launch traced here: 80.4 us
  waiting for transfers between devices  43.4 us (54%)
  Pallas kernels  27.5 us (34%)
  starting transfers between devices  7.32 us (9%)
  other arithmetic  1.4 us (2%)
    all_to_all x1, waiting for transfers between devices, exchange(): got = lax.all_to_all(sent, both, split_axis=0, concat_axis=0, tiled=True)  43.4 us
    pallas_call x1, Pallas kernels, render(): pl.pallas_call(kernel, out_shape=jax.ShapeDtypeStruct((4, groups * sub *...  21 us
    all_to_all x1, starting transfers between devices, exchange(): got = lax.all_to_all(sent, both, split_axis=0, concat_axis=0, tiled=True)  7.32 us
    pallas_call x1, Pallas kernels, pack(): pl.pallas_call(functools.partial(pack_kernel, plan), out_shape=jax.ShapeD...  6.47 us
  transfers between devices with their start and end apart: 1, of which 1 were waited for; matrix products, arithmetic and copies ran while one was open for 0% of the time, Pallas kernels for 0%

profile of v2, /device:TPU:0, one launch (start us, length us, event | category | flops | bytes accessed | tf_op | source)
XLA Modules:
  0.0 80.4 jit_solution(3777307713080337460)
XLA Ops:
  0.0 0.7 pad_add_fusion.1.scalars
  0.7 0.0 copy-start.25
  0.7 0.0 copy-start.4
  0.7 0.0 copy-start.17
  0.7 0.0 copy-start.20
  0.7 6.5 %shard_map.84 = bf16[32,216,128]{2,1,0:T(8,128)(2,1)} custom-call(s32[3]{0:T(128)} %pad_add_fusion.1.scalars, s32[1,1024]{1,0:T(1,128)} %bitcast.100, s32[1,1024]{1,0:T(1,128)} %bitcast.102, s32[1,1024]{1,0:T(1,128)} %bitcast.104, bf16[1024,512]{1,0:T(8,128)(2,1)} %cells_ref.1), custom_call_target="tpu_custom_call" | custom-call | tf_op jit(solution)/shard_map/pallas_call | solution.py:145
  7.1 7.3 %all-to-all-start.1 = ((bf16[32,216,128]{2,1,0:T(8,128)(2,1)}), bf16[32,216,128]{2,1,0:T(8,128)(2,1)S(1)}, u32[]{:S(2)}, u32[]{:S(2)}) async-start(bf16[32,216,128]{2,1,0:T(8,128)(2,1)} %shard_map.84), calls=%async_computation.1 | async-start | bytes 3538944 | tf_op jit(solution)/shard_map/all_to_all | solution.py:318
  14.5 0.0 copy-done.25
  14.5 0.1 select_reduce_fusion
  14.6 43.4 %all-to-all-done.1 = bf16[32,216,128]{2,1,0:T(8,128)(2,1)S(1)} async-done(((bf16[32,216,128]{2,1,0:T(8,128)(2,1)}), bf16[32,216,128]{2,1,0:T(8,128)(2,1)S(1)}, u32[]{:S(2)}, u32[]{:S(2)}) %all-to-all-start.1) | async-done | bytes 1769504 | tf_op jit(solution)/shard_map/all_to_all | solution.py:318
  58.0 0.6 slice_reduce_fusion.1
  59.3 0.0 copy-done.4
  59.3 0.0 copy-done.17
  59.3 0.0 copy-done.20
  59.3 21.1 %conditional.1 = (f32[4,32768]{1,0:T(4,128)}) conditional(s32[]{:T(128)} %convert_element_type.19, (s32[16]{0:T(128)S(1)}, f32[3]{0:T(128)S(1)}, f32[3]{0:T(128)S(1)}, bf16[32,216,128]{2,1,0:T(8,128)(2,1)S(1)}, bf16[512,1024]{1,0:T(8,128)(2,1)S(1)}) %tuple.63, (bf16[32,216,128]{2,1,0:T(8,128)(2,1)S(1)}, s32[]{:T(128)}, s32[1,1024]{1,0:T(1,128)}, ...), branch_computations={%region_2.3_spmd, %region_3.7_spmd} | conditional | flops 6997506048 | bytes 117341648 | solution.py:370
  59.3 21.0 %branch_0_fun.1 = f32[4,32768]{1,0:T(4,128)} custom-call(s32[16]{0:T(128)S(1)} %get-tuple-element.143.brick_of, f32[3]{0:T(128)S(1)} %get-tuple-element.144.gain, f32[3]{0:T(128)S(1)} %get-tuple-element.145.bias, bf16[32,216,128]{2,1,0:T(8,128)(2,1)S(1)} %get-tuple-element.146.recv_ref, bf16[512,1024]{1,0:T(8,128)(2,1)S(1)} %get-tuple-element.147.resample_ref), custom_call_target="tpu_custom_call" | custom-call | tf_op jit(solution)/shard_map/cond/branch_0_fun/pallas_call | solution.py:270
Async XLA Ops:
  0.7 13.8 %copy-start.25 = (s32[16]{0:T(128)S(1)}, s32[16]{0:T(128)}, u32[]{:S(2)}) copy-start(s32[16]{0:T(128)} %param.16) | copy-start | bytes 196
  0.7 58.6 %copy-start.4 = (bf16[512,1024]{1,0:T(8,128)(2,1)S(1)}, bf16[512,1024]{1,0:T(8,128)(2,1)}, u32[]{:S(2)}) copy-start(bf16[512,1024]{1,0:T(8,128)(2,1)} %param.17) | copy-start | bytes 3145732
  0.7 58.6 %copy-start.17 = (f32[3]{0:T(128)S(1)}, f32[3]{0:T(128)}, u32[]{:S(2)}) copy-start(f32[3]{0:T(128)} %param.18) | copy-start | bytes 40
  0.7 58.7 %copy-start.20 = (f32[3]{0:T(128)S(1)}, f32[3]{0:T(128)}, u32[]{:S(2)}) copy-start(f32[3]{0:T(128)} %param.19) | copy-start | bytes 40
  7.1 50.9 %all-to-all-start.1 = ((bf16[32,216,128]{2,1,0:T(8,128)(2,1)}), bf16[32,216,128]{2,1,0:T(8,128)(2,1)S(1)}, u32[]{:S(2)}, u32[]{:S(2)}) async-start(bf16[32,216,128]{2,1,0:T(8,128)(2,1)} %shard_map.84), calls=%async_computation.1 | async-start | bytes 3538944 | tf_op jit(solution)/shard_map/all_to_all | solution.py:318

commit v3 on v2

--- a/solution.py
+++ b/solution.py
@@ -14,9 +14,13 @@
 ID_ROWS = 8
 ID_BASE = 64
 BANDS = 2
+AXES = ("swap", "grp")
+SELECT_ROWS = 1024
 BUCKET_STEP = 8
 LANE_CHUNK = 256
+BRICK_STEP = 16
 LOG2_E = 1.4426950408889634
+EXP2_TOP = 126.0
 
 
 def split(value, size):
@@ -31,20 +35,21 @@
     return jnp.where(same, jnp.bfloat16(1), jnp.bfloat16(0))
 
 
-def route(plan, scalars, dest_ref, tile_ref, counts_ref, cells_ref, slot_ref, tag_ref, masked_ref):
-    owners, capacities, swap_count, layer_tiles, own_tiles, sub = plan
-    block_count, width = cells_ref.shape
+def route(plan, turn, dest_ref, tile_ref, counts_ref, slot_ref, tag_ref):
+    owners, capacities, band_width, swap_count, layer_tiles, own_tiles, sub = plan
+    block_count = dest_ref.shape[1]
+    device = lax.axis_index(AXES)
     group, brick = split(dest_ref[...], swap_count)
     layer, place = split(tile_ref[...], layer_tiles)
     owner, own = split(place, own_tiles)
     own_group, own_sub = split(own, sub)
-    target = group * swap_count + owner
+    target = owner * (owners // swap_count) + group
     row = ((own_group * swap_count + brick) * DEPTH + layer) * sub + own_sub
     parts = [part.astype(jnp.float32) for part in split(row, ID_BASE)]
 
     aimed = lax.broadcasted_iota(jnp.int32, (owners, block_count), 0) == target
     hits = [
-        jnp.where(aimed & (counts_ref[...] > band * (width // BANDS)), 1.0, 0.0)
+        jnp.where(aimed & (counts_ref[...] > band * band_width), 1.0, 0.0)
         for band in range(BANDS)
     ]
     hits = jnp.concatenate(hits, axis=0)
@@ -68,12 +73,12 @@
     tags = jnp.zeros((owners, ID_ROWS, LANES), jnp.float32)
     for band, capacity in enumerate(capacities):
         rows = slice(band * owners, (band + 1) * owners)
-        first = scalars[0] * capacity
+        first = turn * capacity
         order = jnp.sum(before[rows], axis=0, keepdims=True).astype(jnp.int32) - first
-        alive = counts_ref[...] > band * (width // BANDS)
+        alive = counts_ref[...] > band * band_width
         present = alive & (order >= 0) & (order < capacity)
         slot_ref[band : band + 1, :] = jnp.where(present, target * capacity + order, -1)
-        lane = jnp.where(present, (order + scalars[1 + band]) & (LANES - 1), -1)
+        lane = jnp.where(present, (order + device * capacity) & (LANES - 1), -1)
         at_lane = lax.broadcasted_iota(jnp.int32, (LANES, block_count), 0) == lane
         hit = hits[rows].astype(jnp.bfloat16)
         for index, part in enumerate(parts):
@@ -82,29 +87,35 @@
                 hit, placed, (((1,), (1,)), ((), ())), preferred_element_type=jnp.float32
             )
             tags = jnp.where(which == 2 * band + index, spread[:, None, :], tags)
-        more = jnp.max(total[rows]) > (first + capacity).astype(jnp.float32)
+        more = jnp.max(total[rows]) > (jnp.int32(first) + capacity).astype(jnp.float32)
         tags = jnp.where((which == 2 * BANDS + band) & more, 1.0, tags)
     tag_ref[...] = tags.astype(jnp.bfloat16)
 
+
+def mask_dead(counts_ref, cells_ref):
+    block_count, width = cells_ref.shape
     live = jnp.transpose(jnp.broadcast_to(counts_ref[...], (LANES, block_count)))
     lanes = lax.broadcasted_iota(jnp.int32, (block_count, LANES), 1)
     for start in range(0, width, LANES):
         at = pl.ds(start, LANES)
         keep = jnp.where(lanes + start < live, 1.0, 0.0).astype(jnp.bfloat16)
-        masked_ref[:, at] = cells_ref[:, at] * keep
-
-
-def pack_kernel(plan, scalars, dest_ref, tile_ref, counts_ref, cells_ref, out_ref, *scratch):
-    slot_ref, tag_ref, masked_ref = scratch
-    capacities = plan[1]
-    block_count, width = cells_ref.shape
+        cells_ref[:, at] = cells_ref[:, at] * keep
+
+
+def pack_kernel(plan, turn_ref, dest_ref, tile_ref, counts_ref, cells_hbm, out_ref, *scratch):
+    slot_ref, tag_ref, cells_ref, semaphore = scratch
+    capacities, band_width = plan[1:3]
+    block_count = dest_ref.shape[1]
     buckets = out_ref.shape[0]
-    band_width = width // BANDS
     index = pl.program_id(0)
 
     @pl.when(index == 0)
     def _():
-        route(plan, scalars, dest_ref, tile_ref, counts_ref, cells_ref, *scratch)
+        copy = pltpu.make_async_copy(cells_hbm, cells_ref, semaphore)
+        copy.start()
+        route(plan, turn_ref[0], dest_ref, tile_ref, counts_ref, slot_ref, tag_ref)
+        copy.wait()
+        mask_dead(counts_ref, cells_ref)
 
     top = 0
     for band, capacity in enumerate(capacities):
@@ -119,7 +130,7 @@
             )
             picked = jnp.dot(
                 pick,
-                masked_ref[:, band * band_width : (band + 1) * band_width],
+                cells_ref[:, band * band_width : (band + 1) * band_width],
                 preferred_element_type=jnp.float32,
             ).astype(jnp.bfloat16)
             for bucket in range(rows // capacity):
@@ -134,13 +145,11 @@
     out_ref[:, top:, :] = tag_ref[pl.ds(index * buckets, buckets)]
 
 
-def pack(plan, turn, my_index, dest, tile, counts, cells):
-    owners, capacities = plan[:2]
-    block_count, width = cells.shape
-    rows = width // BANDS // LANES * sum(capacities) + ID_ROWS
+def pack(plan, turn, dest, tile, counts, cells):
+    owners, capacities, band_width = plan[:3]
+    block_count = cells.shape[0]
+    rows = band_width // LANES * sum(capacities) + ID_ROWS
     buckets = min(BUCKET_STEP, owners)
-    offsets = [my_index * capacity % LANES for capacity in capacities]
-    scalars = jnp.stack([turn, *offsets]).astype(jnp.int32)
     row = pl.BlockSpec((1, block_count), lambda i, *_: (0, 0))
     return pl.pallas_call(
         functools.partial(pack_kernel, plan),
@@ -148,61 +157,78 @@
         grid_spec=pltpu.PrefetchScalarGridSpec(
             num_scalar_prefetch=1,
             grid=(owners // buckets,),
-            in_specs=[row, row, row, pl.BlockSpec((block_count, width), lambda i, *_: (0, 0))],
+            in_specs=[row, row, row, pl.BlockSpec(memory_space=pl.ANY)],
             out_specs=pl.BlockSpec((buckets, rows, LANES), lambda i, *_: (i, 0, 0)),
             scratch_shapes=[
                 pltpu.VMEM((8, block_count), jnp.int32),
                 pltpu.VMEM((owners, ID_ROWS, LANES), jnp.bfloat16),
-                pltpu.VMEM((block_count, width), cells.dtype),
+                pltpu.VMEM(cells.shape, cells.dtype),
+                pltpu.SemaphoreType.DMA,
             ],
         ),
-    )(scalars, dest, tile, counts, cells)
-
-
-def integrate(sample_ref, out_ref, start, brick_of, gain, bias, opacity_step, bricks, rows):
+    )(jnp.full((1,), turn, jnp.int32), dest, tile, counts, cells)
+
+
+def integrate_bricks(sample_ref, places, state, brick_of, gain, bias, opacity_step, rows):
     sub = rows // DEPTH
-    chunk = sample_ref.shape[1]
     half_gain = [0.5 * gain[k] for k in range(3)]
     half_bias = [0.5 * bias[k] for k in range(3)]
-
-    def brick_step(place, carry):
-        transmit, colors = carry[0], list(carry[1:])
+    transmit, *colors = state
+    for place in places:
         top = brick_of[place] * rows
         for layer in range(DEPTH):
             v = sample_ref[pl.ds(pl.multiple_of(top + layer * sub, sub), sub), :]
             scaled = v * LOG2_E
-            softplus = jnp.maximum(scaled, 0.0) + jnp.log2(1.0 + jnp.exp2(-jnp.abs(scaled)))
+            softplus = jnp.log2(1.0 + jnp.exp2(jnp.minimum(scaled, EXP2_TOP)))
+            softplus = jnp.maximum(scaled, softplus)
             passed = transmit * jnp.exp2(-opacity_step * softplus)
             weight = transmit - passed
             for k in range(3):
                 colors[k] = colors[k] + weight * jnp.tanh(half_gain[k] * v + half_bias[k])
             transmit = passed
-        return (transmit, *colors)
+    return (transmit, *colors)
+
+
+def integrate(sample_ref, out_ref, start, scene, beside=None):
+    brick_of, gain, bias, opacity_step, bricks, rows = scene
+    sub = rows // DEPTH
+    chunk = sample_ref.shape[1]
+    at_once = min(BRICK_STEP, bricks)
+    steps = bricks // at_once
+
+    def step(index, state):
+        if beside is not None:
+            beside(index, steps)
+        places = [index * at_once + place for place in range(at_once)]
+        return integrate_bricks(sample_ref, places, state, brick_of, gain, bias, opacity_step, rows)
 
     zero = jnp.zeros((sub, chunk), jnp.float32)
-    done = lax.fori_loop(0, bricks, brick_step, (zero + 1.0, zero, zero, zero), unroll=4)
-    opacity = 1.0 - done[0]
-    planes = [0.5 * (opacity + done[1 + k]) for k in range(3)] + [opacity]
+    state = (zero + 1.0, zero, zero, zero)
+    if steps == 1:
+        state = step(0, state)
+    else:
+        state = lax.fori_loop(0, steps, step, state)
+    opacity = 1.0 - state[0]
+    planes = [0.5 * (opacity + state[1 + k]) for k in range(3)] + [opacity]
     for k, plane in enumerate(planes):
         for row in range(sub):
             at = pl.ds(start + row * (out_ref.shape[1] // sub), chunk)
             out_ref[k : k + 1, at] = plane[row : row + 1]
 
 
-def resample_and_integrate(read, resample_ref, out_ref, sample_ref, *scene):
-    for start in range(0, resample_ref.shape[1], LANE_CHUNK):
-        sample_ref[...] = jnp.dot(
-            read(), resample_ref[:, start : start + LANE_CHUNK], preferred_element_type=jnp.float32
-        )
-        integrate(sample_ref, out_ref, start, *scene)
+def resample_chunk(cells, rows, resample_ref, chunk, sample_ref):
+    columns = resample_ref[:, chunk * LANE_CHUNK : (chunk + 1) * LANE_CHUNK]
+    sample_ref[rows, :] = jnp.dot(cells, columns, preferred_element_type=jnp.float32)
 
 
 def render_kernel(
     opacity_step, bricks, brick_of, gain, bias, cells_ref, resample_ref, out_ref, sample_ref
 ):
-    rows = cells_ref.shape[1] // bricks
-    scene = (brick_of, gain, bias, opacity_step, bricks, rows)
-    resample_and_integrate(lambda: cells_ref[0], resample_ref, out_ref, sample_ref, *scene)
+    group_rows = cells_ref.shape[1]
+    scene = (brick_of, gain, bias, opacity_step, bricks, group_rows // bricks)
+    for chunk in range(resample_ref.shape[1] // LANE_CHUNK):
+        resample_chunk(cells_ref[0], slice(0, group_rows), resample_ref, chunk, sample_ref)
+        integrate(sample_ref, out_ref, chunk * LANE_CHUNK, scene)
 
 
 def unpack(capacities, recv_ref, data_refs, id_refs):
@@ -233,10 +259,20 @@
             id_ref[0:1, low:high] = row.astype(jnp.int32)
 
 
+def select_rows(rows, data_refs, id_refs, tile_ref):
+    for band, (data_ref, id_ref) in enumerate(zip(data_refs, id_refs)):
+        slots, width = data_ref.shape
+        pick = one_hot(rows.size, slots, rows.start, id_ref[0:1, :])
+        tile_ref[rows, band * width : (band + 1) * width] = jnp.dot(
+            pick, data_ref[...], preferred_element_type=jnp.float32
+        ).astype(jnp.bfloat16)
+
+
 def gather_render_kernel(
     opacity_step,
     bricks,
     capacities,
+    groups,
     brick_of,
     gain,
     bias,
@@ -246,23 +282,37 @@
     *scratch,
 ):
     data_refs, id_refs = scratch[:BANDS], scratch[BANDS : 2 * BANDS]
-    tile_ref, sample_ref = scratch[2 * BANDS :]
-    group_rows = tile_ref.shape[0]
-
-    @pl.when(pl.program_id(0) == 0)
+    tile_ref, *sample_refs = scratch[2 * BANDS :]
+    chunks = resample_ref.shape[1] // LANE_CHUNK
+    group_rows = sample_refs[0].shape[0]
+    group = pl.program_id(0)
+
+    def part_of(index, size):
+        return pl.ds(pl.multiple_of(index * size, size), size)
+
+    @pl.when(group == 0)
     def _():
         unpack(capacities, recv_ref, data_refs, id_refs)
 
-    band_width = data_refs[0].shape[1]
-    for band, (data_ref, id_ref) in enumerate(zip(data_refs, id_refs)):
-        pick = one_hot(
-            group_rows, data_ref.shape[0], pl.program_id(0) * group_rows, id_ref[0:1, :]
-        )
-        tile_ref[:, band * band_width : (band + 1) * band_width] = jnp.dot(
-            pick, data_ref[...], preferred_element_type=jnp.float32
-        ).astype(jnp.bfloat16)
+        def start(index, _):
+            select_rows(part_of(index, SELECT_ROWS), data_refs, id_refs, tile_ref)
+            return 0
+
+        lax.fori_loop(0, tile_ref.shape[0] // SELECT_ROWS, start, 0)
+
+    def resample(rows, chunk):
+        at = pl.ds(pl.multiple_of(group * group_rows + rows.start, rows.size), rows.size)
+        resample_chunk(tile_ref[at, :], rows, resample_ref, chunk, sample_refs[chunk % 2])
+
+    resample(pl.ds(0, group_rows), 0)
     scene = (brick_of, gain, bias, opacity_step, bricks, group_rows // bricks)
-    resample_and_integrate(lambda: tile_ref[...], resample_ref, out_ref, sample_ref, *scene)
+    for chunk in range(chunks):
+
+        def beside(index, steps):
+            if chunk + 1 < chunks:
+                resample(part_of(index, group_rows // steps), chunk + 1)
+
+        integrate(sample_refs[chunk % 2], out_ref, chunk * LANE_CHUNK, scene, beside)
 
 
 def render(kernel, source, source_spec, groups, group_rows, bricks, sub, scene, resample, scratch):
@@ -289,8 +339,7 @@
 
 
 def on_device(cells, counts, donor_dest, donor_tile, depth_rank, resample, color_gain, color_bias):
-    both = ("grp", "swap")
-    owners = lax.axis_size(both)
+    owners = lax.axis_size(AXES)
     group_count = lax.axis_size("grp")
     swap_count = lax.axis_size("swap")
     block_count, block_width = cells.shape
@@ -304,18 +353,17 @@
     opacity_step = 2.5 / (DEPTH * swap_count)
     mean = block_count / owners
     capacities = (slots_for(mean, owners, 5.5), slots_for(mean * 4 / 7, owners, 5.0))
-    plan = (owners, capacities, swap_count, layer_tiles, own_tiles, sub)
     band_width = block_width // BANDS
-
-    my_index = lax.axis_index(both)
+    plan = (owners, capacities, band_width, swap_count, layer_tiles, own_tiles, sub)
+
     dest_row = donor_dest.reshape(1, block_count)
     tile_row = donor_tile.reshape(1, block_count)
     counts_row = counts.reshape(1, block_count)
     tag_row = band_width // LANES * sum(capacities)
 
     def exchange(turn):
-        sent = pack(plan, turn, my_index, dest_row, tile_row, counts_row, cells)
-        got = lax.all_to_all(sent, both, split_axis=0, concat_axis=0, tiled=True)
+        sent = pack(plan, turn, dest_row, tile_row, counts_row, cells)
+        got = lax.all_to_all(sent, AXES, split_axis=0, concat_axis=0, tiled=True)
         flags = got[:, tag_row + 2 * BANDS : tag_row + 3 * BANDS, 0]
         return got, jnp.max(flags) > 0
 
@@ -344,11 +392,12 @@
     received, more = exchange(jnp.int32(0))
 
     def one_round():
-        kernel = functools.partial(gather_render_kernel, opacity_step, swap_count, capacities)
+        kernel = functools.partial(gather_render_kernel, opacity_step, swap_count, capacities, groups)
         slots = [owners * capacity for capacity in capacities]
         scratch = [pltpu.VMEM((count, band_width), jnp.bfloat16) for count in slots]
         scratch += [pltpu.VMEM((8, count), jnp.int32) for count in slots]
-        scratch += [pltpu.VMEM((group_rows, block_width), jnp.bfloat16)]
+        scratch += [pltpu.VMEM((groups * group_rows, block_width), jnp.bfloat16)]
+        scratch += [pltpu.VMEM((group_rows, LANE_CHUNK), jnp.float32)]
         whole = pl.BlockSpec(received.shape, lambda i, *_: (0, 0, 0))
         shape = (groups, group_rows, swap_count, sub)
         return render(kernel, received, whole, *shape, scene, resample, scratch)

time: 80.6 us -> 71.7 us (0.89)
  Pallas kernels: 27.5 us -> 21.1 us
  waiting for transfers between devices: 43.4 us -> 41.6 us
    pallas_call x1, Pallas kernels: 21 us -> 15.3 us  [render(): pl.pallas_call(kernel, out_shape=jax.ShapeDtypeStruct((4, groups * sub *...]
    all_to_all x1, waiting for transfers between devices: 43.4 us -> 41.6 us  [exchange(): got = lax.all_to_all(sent, AXES, split_axis=0, concat_axis=0, tiled=True)]
where the time goes in v3:
time: 71.7 us; the launch traced here: 71.5 us
  waiting for transfers between devices  41.6 us (58%)
  Pallas kernels  21.1 us (29%)
  starting transfers between devices  7.34 us (10%)
  other arithmetic  0.75 us (1%)
    all_to_all x1, waiting for transfers between devices, exchange(): got = lax.all_to_all(sent, AXES, split_axis=0, concat_axis=0, tiled=True)  41.6 us
    pallas_call x1, Pallas kernels, render(): pl.pallas_call(kernel, out_shape=jax.ShapeDtypeStruct((4, groups * sub *...  15.3 us
    all_to_all x1, starting transfers between devices, exchange(): got = lax.all_to_all(sent, AXES, split_axis=0, concat_axis=0, tiled=True)  7.34 us
    pallas_call x1, Pallas kernels, pack(): pl.pallas_call(functools.partial(pack_kernel, plan), out_shape=jax.ShapeD...  5.83 us
  transfers between devices with their start and end apart: 1, of which 1 were waited for; matrix products, arithmetic and copies ran while one was open for 0% of the time, Pallas kernels for 0%

profile of v3, /device:TPU:0, one launch (start us, length us, event | category | flops | bytes accessed | tf_op | source)
XLA Modules:
  0.0 71.5 jit_solution(4093322272156977200)
XLA Ops:
  0.0 0.0 copy-start.21
  0.0 0.0 copy-start.4
  0.0 0.0 copy-start.13
  0.0 0.0 copy-start.16
  0.0 5.8 %shard_map.84 = bf16[32,216,128]{2,1,0:T(8,128)(2,1)} custom-call(s32[1]{0:T(128)} %constant.162.clone.1.turn_ref, s32[1,1024]{1,0:T(1,128)} %bitcast.90, s32[1,1024]{1,0:T(1,128)} %bitcast.92, s32[1,1024]{1,0:T(1,128)} %bitcast.94, bf16[1024,512]{1,0:T(8,128)(2,1)} %cells_hbm.1), custom_call_target="tpu_custom_call" | custom-call | tf_op jit(solution)/shard_map/pallas_call | solution.py:154
  5.9 7.3 %all-to-all-start.1 = ((bf16[32,216,128]{2,1,0:T(8,128)(2,1)}), bf16[32,216,128]{2,1,0:T(8,128)(2,1)S(1)}, u32[]{:S(2)}, u32[]{:S(2)}) async-start(bf16[32,216,128]{2,1,0:T(8,128)(2,1)} %shard_map.84), calls=%async_computation.1 | async-start | bytes 3538944 | tf_op jit(solution)/shard_map/all_to_all | solution.py:366
  13.2 0.0 copy-done.21
  13.2 0.1 select_reduce_fusion
  13.3 41.6 %all-to-all-done.1 = bf16[32,216,128]{2,1,0:T(8,128)(2,1)S(1)} async-done(((bf16[32,216,128]{2,1,0:T(8,128)(2,1)}), bf16[32,216,128]{2,1,0:T(8,128)(2,1)S(1)}, u32[]{:S(2)}, u32[]{:S(2)}) %all-to-all-start.1) | async-done | bytes 1769504 | tf_op jit(solution)/shard_map/all_to_all | solution.py:366
  54.9 0.6 slice_reduce_fusion.1
  56.2 0.0 copy-done.4
  56.2 0.0 copy-done.13
  56.2 0.0 copy-done.16
  56.2 15.3 %conditional.1 = (f32[4,32768]{1,0:T(4,128)}) conditional(s32[]{:T(128)} %convert_element_type.19, (s32[16]{0:T(128)S(1)}, f32[3]{0:T(128)S(1)}, f32[3]{0:T(128)S(1)}, bf16[32,216,128]{2,1,0:T(8,128)(2,1)S(1)}, bf16[512,1024]{1,0:T(8,128)(2,1)S(1)}) %tuple.63, (bf16[32,216,128]{2,1,0:T(8,128)(2,1)S(1)}, s32[1,1024]{1,0:T(1,128)}, ...), branch_computations={%region_2.3_spmd, %region_3.7_spmd} | conditional | flops 6997506048 | bytes 117234768 | solution.py:419
  56.2 15.3 %branch_0_fun.1 = f32[4,32768]{1,0:T(4,128)} custom-call(s32[16]{0:T(128)S(1)} %get-tuple-element.112.brick_of, f32[3]{0:T(128)S(1)} %get-tuple-element.113.gain, f32[3]{0:T(128)S(1)} %get-tuple-element.114.bias, bf16[32,216,128]{2,1,0:T(8,128)(2,1)S(1)} %get-tuple-element.115.recv_ref, bf16[512,1024]{1,0:T(8,128)(2,1)S(1)} %get-tuple-element.116.resample_ref), custom_call_target="tpu_custom_call" | custom-call | tf_op jit(solution)/shard_map/cond/branch_0_fun/pallas_call | solution.py:320
Async XLA Ops:
  0.0 13.2 %copy-start.21 = (s32[16]{0:T(128)S(1)}, s32[16]{0:T(128)}, u32[]{:S(2)}) copy-start(s32[16]{0:T(128)} %param.16) | copy-start | bytes 196
  0.0 56.2 %copy-start.4 = (bf16[512,1024]{1,0:T(8,128)(2,1)S(1)}, bf16[512,1024]{1,0:T(8,128)(2,1)}, u32[]{:S(2)}) copy-start(bf16[512,1024]{1,0:T(8,128)(2,1)} %param.17) | copy-start | bytes 3145732
  0.0 56.2 %copy-start.13 = (f32[3]{0:T(128)S(1)}, f32[3]{0:T(128)}, u32[]{:S(2)}) copy-start(f32[3]{0:T(128)} %param.18) | copy-start | bytes 40
  0.0 56.2 %copy-start.16 = (f32[3]{0:T(128)S(1)}, f32[3]{0:T(128)}, u32[]{:S(2)}) copy-start(f32[3]{0:T(128)} %param.19) | copy-start | bytes 40
  5.9 49.0 %all-to-all-start.1 = ((bf16[32,216,128]{2,1,0:T(8,128)(2,1)}), bf16[32,216,128]{2,1,0:T(8,128)(2,1)S(1)}, u32[]{:S(2)}, u32[]{:S(2)}) async-start(bf16[32,216,128]{2,1,0:T(8,128)(2,1)} %shard_map.84), calls=%async_computation.1 | async-start | bytes 3538944 | tf_op jit(solution)/shard_map/all_to_all | solution.py:366

commit v4 on v3

v4 whole, which is shorter than its diff:
```python
import functools

import jax
import jax.numpy as jnp
from jax import lax
from jax.experimental import pallas as pl
from jax.experimental.pallas import tpu as pltpu
from jax.sharding import PartitionSpec as P

IMG_W = 1024
IMG_H = 1024
DEPTH = 4
LANES = 128
MORE = 512.0
NO_LABEL = -4096.0
BANDS = 2
AXES = ("swap", "grp")
SELECT_ROWS = 384
STEP_ROWS = 256
BUCKET_STEP = 8
LOG2_E = 1.4426950408889634
EXP2_TOP = 126.0


def split(value, size):
    if size & (size - 1) == 0:
        return jnp.right_shift(value, size.bit_length() - 1), value & (size - 1)
    return value // size, value % size


def usable_slots(band, capacity):
    return capacity - 1 if band == BANDS - 1 else capacity


def one_hot(rows, columns, start, labels):
    row = (lax.broadcasted_iota(jnp.int32, (rows, columns), 0) + start).astype(jnp.int16)
    same = row == jnp.broadcast_to(labels.astype(jnp.int16), (rows, columns))
    return jnp.where(same, jnp.bfloat16(1), jnp.bfloat16(0))


def route(plan, turn, dest_ref, tile_ref, counts_ref, slot_ref, tag_ref):
    owners, capacities, band_width, swap_count, layer_tiles, own_tiles = plan
    block_count = dest_ref.shape[1]
    device = lax.axis_index(AXES)
    group, brick = split(dest_ref[...], swap_count)
    layer, place = split(tile_ref[...], layer_tiles)
    owner, own = split(place, own_tiles)
    target = owner * (owners // swap_count) + group
    parts = [own.astype(jnp.float32), (brick * DEPTH + layer).astype(jnp.float32)]

    aimed = lax.broadcasted_iota(jnp.int32, (owners, block_count), 0) == target
    hits = [
        jnp.where(aimed & (counts_ref[...] > band * band_width), 1.0, 0.0)
        for band in range(BANDS)
    ]
    hits = jnp.concatenate(hits, axis=0)
    step = min(256, block_count)
    earlier = lax.broadcasted_iota(jnp.int32, (step, step), 0) < lax.broadcasted_iota(
        jnp.int32, (step, step), 1
    )
    earlier = jnp.where(earlier, 1.0, 0.0).astype(jnp.bfloat16)
    total = jnp.zeros((BANDS * owners, 1), jnp.float32)
    before = []
    for start in range(0, block_count, step):
        part = hits[:, start : start + step]
        before.append(
            total
            + jnp.dot(part.astype(jnp.bfloat16), earlier, preferred_element_type=jnp.float32)
        )
        total = total + jnp.sum(part, axis=1, keepdims=True)
    before = jnp.concatenate(before, axis=1) * hits

    lanes = lax.broadcasted_iota(jnp.int32, (LANES, block_count), 0)
    lane_of = lax.broadcasted_iota(jnp.int32, (1, LANES), 1)
    for band, capacity in enumerate(capacities):
        rows = slice(band * owners, (band + 1) * owners)
        usable = usable_slots(band, capacity)
        first = turn * usable
        order = jnp.sum(before[rows], axis=0, keepdims=True).astype(jnp.int32) - first
        alive = counts_ref[...] > band * band_width
        present = alive & (order >= 0) & (order < usable)
        slot_ref[band : band + 1, :] = jnp.where(present, target * capacity + order, -1)
        placed = jnp.zeros((LANES, block_count), jnp.float32)
        for index, part in enumerate(parts):
            lane = (order + device * capacity + index * capacity) & (LANES - 1)
            placed = jnp.where(lanes == jnp.where(present, lane, -1), part, placed)
        tags = lax.dot_general(
            hits[rows].astype(jnp.bfloat16),
            placed.astype(jnp.bfloat16),
            (((1,), (1,)), ((), ())),
            preferred_element_type=jnp.float32,
        )
        more = jnp.max(total[rows]) > (jnp.int32(first) + usable).astype(jnp.float32)
        flag_lane = (device * capacity + 2 * capacity) & (LANES - 1)
        if band == BANDS - 1:
            more = more | more_before
            tags = tags + jnp.where((lane_of == flag_lane) & more, MORE, 0.0)
        more_before = more
        tag_ref[:, band * LANES : (band + 1) * LANES] = tags


def mask_dead(counts_ref, cells_ref):
    block_count, width = cells_ref.shape
    live = jnp.transpose(jnp.broadcast_to(counts_ref[...], (LANES, block_count)))
    lanes = lax.broadcasted_iota(jnp.int32, (block_count, LANES), 1)
    for start in range(0, width, LANES):
        at = pl.ds(start, LANES)
        keep = jnp.where(lanes + start < live, 1.0, 0.0).astype(jnp.bfloat16)
        cells_ref[:, at] = cells_ref[:, at] * keep


def pack_kernel(plan, turn_refs, dest_ref, tile_ref, counts_ref, cells_hbm, out_ref, *scratch):
    slot_ref, tag_ref, cells_ref, semaphore = scratch
    capacities, band_width = plan[1:3]
    block_count = dest_ref.shape[1]
    buckets = out_ref.shape[0]
    index = pl.program_id(0)

    @pl.when(index == 0)
    def _():
        copy = pltpu.make_async_copy(cells_hbm, cells_ref, semaphore)
        copy.start()
        turn = turn_refs[0][0] if turn_refs else 0
        route(plan, turn, dest_ref, tile_ref, counts_ref, slot_ref, tag_ref)
        copy.wait()
        mask_dead(counts_ref, cells_ref)

    top = 0
    for band, capacity in enumerate(capacities):
        at_once = max(1, min(buckets, 512 // capacity))
        for base in range(0, buckets, at_once):
            rows = min(at_once, buckets - base) * capacity
            pick = one_hot(
                rows,
                block_count,
                (index * buckets + base) * capacity,
                slot_ref[band : band + 1, :],
            )
            picked = jnp.dot(
                pick,
                cells_ref[:, band * band_width : (band + 1) * band_width],
                preferred_element_type=jnp.float32,
            )
            if band == BANDS - 1:
                first = pl.multiple_of(index * buckets, buckets) + base
                tags = tag_ref[pl.ds(first, rows // capacity), :]
                place = lax.broadcasted_iota(jnp.int32, (rows // capacity, capacity, 1), 1)
                tags = jnp.where(place == capacity - 1, tags[:, None, :], 0.0)
                picked = picked + tags.reshape(rows, BANDS * LANES)
            picked = picked.astype(jnp.bfloat16)
            for bucket in range(rows // capacity):
                for column in range(band_width // LANES):
                    out_ref[base + bucket, top + column * capacity : top + (column + 1) * capacity] = (
                        picked[
                            bucket * capacity : (bucket + 1) * capacity,
                            column * LANES : (column + 1) * LANES,
                        ]
                    )
        top += band_width // LANES * capacity


def pack(plan, turns, dest, tile, counts, cells):
    owners, capacities, band_width = plan[:3]
    block_count = cells.shape[0]
    rows = band_width // LANES * sum(capacities)
    buckets = min(BUCKET_STEP, owners)
    row = pl.BlockSpec((1, block_count), lambda i, *_: (0, 0))
    return pl.pallas_call(
        lambda *refs: pack_kernel(plan, refs[: len(turns)], *refs[len(turns) :]),
        out_shape=jax.ShapeDtypeStruct((owners, rows, LANES), cells.dtype),
        grid_spec=pltpu.PrefetchScalarGridSpec(
            num_scalar_prefetch=len(turns),
            grid=(owners // buckets,),
            in_specs=[row, row, row, pl.BlockSpec(memory_space=pl.ANY)],
            out_specs=pl.BlockSpec((buckets, rows, LANES), lambda i, *_: (i, 0, 0)),
            scratch_shapes=[
                pltpu.VMEM((8, block_count), jnp.int32),
                pltpu.VMEM((owners, BANDS * LANES), jnp.float32),
                pltpu.VMEM(cells.shape, cells.dtype),
                pltpu.SemaphoreType.DMA,
            ],
        ),
    )(*turns, dest, tile, counts, cells)


def integrate(sample_ref, empty_ref, out_ref, group, blocks, positions, gain, bias, opacity_step):
    tiles, span = empty_ref.shape[1], sample_ref.shape[1]
    sub = out_ref.shape[1] // span
    steps = STEP_ROWS // tiles
    half_gain = [0.5 * gain[k] for k in range(3)]
    half_bias = [0.5 * bias[k] for k in range(3)]

    def block_step(block, state):
        passing, fed, *colors = state
        for inside in range(steps):
            step = block * steps + inside
            at = pl.multiple_of(step * tiles + group * sub, sub)
            v = sample_ref[pl.ds(at, sub), :]
            empty = empty_ref[step, pl.ds(pl.multiple_of(group * sub, sub), sub), :]
            empty = jnp.concatenate([empty] * (span // LANES), axis=1)
            scaled = v * LOG2_E
            softplus = jnp.log2(1.0 + jnp.exp2(jnp.minimum(scaled, EXP2_TOP)))
            softplus = jnp.maximum(scaled, softplus)
            passed = passing * jnp.exp2(-opacity_step * softplus)
            weight = (passing - passed) * empty
            fed = fed + weight
            for k in range(3):
                colors[k] = colors[k] + weight * jnp.tanh(half_gain[k] * v + half_bias[k])
            passing = passed
        return (passing, fed, *colors)

    zero = jnp.zeros((sub, span), jnp.float32)
    passing, fed, *colors = lax.fori_loop(0, blocks, block_step, (zero + 1.0, zero) + (zero,) * 3)
    left = (positions - blocks * steps).astype(jnp.float32)
    opacity = 1.0 - passing * jnp.exp2(zero - opacity_step * left)
    rest = opacity - fed
    planes = [
        0.5 * (opacity + colors[k] + rest * jnp.tanh(zero + half_bias[k])) for k in range(3)
    ] + [opacity]
    for k, plane in enumerate(planes):
        for row in range(sub):
            out_ref[k : k + 1, row * span : (row + 1) * span] = plane[row : row + 1]


def render_kernel(
    opacity_step, positions, _, gain, bias, cells_ref, resample_ref, out_ref, sample_ref, empty_ref
):
    group = pl.program_id(0)
    tiles = empty_ref.shape[1]

    @pl.when(group == 0)
    def _():
        empty_ref[...] = jnp.ones(empty_ref.shape, jnp.float32)

        def resample(block, _):
            rows = pl.ds(pl.multiple_of(block * STEP_ROWS, STEP_ROWS), STEP_ROWS)
            sample_ref[rows, :] = jnp.dot(
                cells_ref[rows, :], resample_ref[...], preferred_element_type=jnp.float32
            )
            return 0

        lax.fori_loop(0, cells_ref.shape[0] // STEP_ROWS, resample, 0)

    blocks = jnp.int32(positions * tiles // STEP_ROWS)
    integrate(
        sample_ref, empty_ref, out_ref, group, blocks, positions, gain, bias, opacity_step
    )


def label_rows(tags, capacity):
    owners = tags.shape[0]
    lane = lax.broadcasted_iota(jnp.int32, (1, LANES), 1)
    blocks = []
    for block in range(owners * capacity // LANES):
        low, high = block * LANES, (block + 1) * LANES
        row = jnp.zeros((1, LANES), jnp.float32)
        for source in range(low // capacity, -(-high // capacity)):
            part = tags[source : source + 1]
            if source * capacity < low:
                part = jnp.where(lane < (source + 1) * capacity - low, part, 0.0)
            elif (source + 1) * capacity > high:
                part = jnp.where(lane >= source * capacity - low, part, 0.0)
            row = row + part
        blocks.append(row)
    return jnp.concatenate(blocks, axis=1)


def unpack(
    capacities, positions, tiles, mask, opacity_step, recv_ref, data_refs, id_refs, *counted
):
    empty_ref, block_ref = counted
    owners = recv_ref.shape[0]
    top = 0
    for capacity, data_ref in zip(capacities, data_refs):
        for column in range(data_ref.shape[1] // LANES):
            for source in range(owners):
                data_ref[
                    source * capacity : (source + 1) * capacity,
                    column * LANES : (column + 1) * LANES,
                ] = recv_ref[source, top : top + capacity, :]
            top += capacity
    rows, at_tile, at_position = [], [], []
    lane = lax.broadcasted_iota(jnp.int32, (owners, LANES), 1)
    source = lax.broadcasted_iota(jnp.int32, (owners, LANES), 0)
    first_label = top - (BANDS - 1) * capacities[-1] - 1
    for band, capacity in enumerate(capacities):
        tags = recv_ref[:, first_label + band * capacities[-1], :].astype(jnp.float32)
        usable = usable_slots(band, capacity)
        place = (lane - source * capacity) & (LANES - 1)
        tile = jnp.where(place < usable, tags, jnp.where(place < capacity, NO_LABEL, 0.0))
        position = pltpu.roll(tags, LANES - capacity, 1)
        position = jnp.where(place < usable, position, 0.0)
        tile, position = label_rows(tile, capacity), label_rows(position, capacity)
        rows.append(tile)
        at_tile.append(one_hot(tiles, owners * capacity, 0, tile.astype(jnp.int32)))
        at_position.append(one_hot(positions, owners * capacity, 0, position.astype(jnp.int32) ^ mask))
    hits = lax.dot_general(
        at_position[0],
        at_tile[0],
        (((1,), (1,)), ((), ())),
        preferred_element_type=jnp.float32,
    )
    is_fed = jnp.where(hits > 0.0, 1.0, 0.0)
    earlier = lax.broadcasted_iota(jnp.int32, (positions, positions), 1) < lax.broadcasted_iota(
        jnp.int32, (positions, positions), 0
    )
    earlier = jnp.where(earlier, 1.0, 0.0).astype(jnp.bfloat16)
    number = jnp.dot(earlier, is_fed.astype(jnp.bfloat16), preferred_element_type=jnp.float32)
    for band, id_ref in enumerate(id_refs):
        step = jnp.dot(
            number.astype(jnp.bfloat16), at_tile[band], preferred_element_type=jnp.float32
        )
        step = jnp.sum(step * at_position[band].astype(jnp.float32), axis=0, keepdims=True)
        id_ref[0:1, :] = (step * tiles + rows[band]).astype(jnp.int32)

    total = jnp.sum(is_fed, axis=0, keepdims=True)
    groups = block_ref.shape[0] - 1
    for index in range(groups):
        part = total[:, index * tiles // groups : (index + 1) * tiles // groups]
        block_ref[index] = -(-jnp.max(part).astype(jnp.int32) // (STEP_ROWS // tiles))
    block_ref[groups] = -(-jnp.max(total).astype(jnp.int32) // (SELECT_ROWS // tiles))

    hits = lax.dot_general(
        at_tile[0],
        at_position[0],
        (((1,), (1,)), ((), ())),
        preferred_element_type=jnp.float32,
    )
    until = lax.broadcasted_iota(jnp.int32, (positions, positions), 0) <= lax.broadcasted_iota(
        jnp.int32, (positions, positions), 1
    )
    until = jnp.where(until, 1.0, 0.0).astype(jnp.bfloat16)
    through = jnp.where(hits > 0.0, 1.0, 0.0).astype(jnp.bfloat16)
    through = jnp.dot(through, until, preferred_element_type=jnp.float32)
    step = lax.broadcasted_iota(jnp.int32, (positions, tiles, positions), 0).astype(jnp.float32)
    passed_over = jnp.where(through[None] <= step, 1.0, 0.0)
    passed_over = passed_over.reshape(positions * tiles, positions).astype(jnp.bfloat16)
    every = jnp.ones((positions, LANES), jnp.bfloat16)
    place = jnp.dot(passed_over, every, preferred_element_type=jnp.float32)
    place = place.reshape(positions, tiles, LANES)
    step = lax.broadcasted_iota(jnp.int32, (positions, tiles, LANES), 0).astype(jnp.float32)
    before = jnp.exp2(-opacity_step * (place - step))
    empty_ref[...] = jnp.where(place < positions, before, 0.0)


def gather_render_kernel(
    opacity_step,
    positions,
    capacities,
    depth_rank,
    gain,
    bias,
    recv_ref,
    resample_ref,
    out_ref,
    sample_ref,
    empty_ref,
    *scratch,
):
    data_refs, id_refs = scratch[:BANDS], scratch[BANDS : 2 * BANDS]
    tile_ref, block_ref = scratch[2 * BANDS :]
    group = pl.program_id(0)
    groups = block_ref.shape[0] - 1
    band_width = data_refs[0].shape[1]

    @pl.when(group == 0)
    def _():
        unpack(
            capacities,
            positions,
            empty_ref.shape[1],
            depth_rank[0] * DEPTH,
            opacity_step,
            recv_ref,
            data_refs,
            id_refs,
            empty_ref,
            block_ref,
        )

        def select(block, _):
            start = pl.multiple_of(block * SELECT_ROWS, SELECT_ROWS)
            for band, (data_ref, id_ref) in enumerate(zip(data_refs, id_refs)):
                pick = one_hot(SELECT_ROWS, data_ref.shape[0], start, id_ref[0:1, :])
                tile_ref[:, band * band_width : (band + 1) * band_width] = jnp.dot(
                    pick, data_ref[...], preferred_element_type=jnp.float32
                ).astype(jnp.bfloat16)

            def resample(part, _):
                near = pl.ds(pl.multiple_of(part * (SELECT_ROWS // 2), 16), SELECT_ROWS // 2)
                far = start + part * (SELECT_ROWS // 2)
                far = pl.ds(pl.multiple_of(far, 16), SELECT_ROWS // 2)
                sample_ref[far, :] = jnp.dot(
                    tile_ref[near, :], resample_ref[...], preferred_element_type=jnp.float32
                )
                return 0

            lax.fori_loop(0, 2, resample, 0)
            return 0

        lax.fori_loop(0, block_ref[groups], select, 0)

    blocks = block_ref[group]
    integrate(
        sample_ref, empty_ref, out_ref, group, blocks, positions, gain, bias, opacity_step
    )


def render(kernel, source, tiles, positions, scene, resample, scratch):
    width, tile_span = resample.shape
    sub = min(8, tiles)
    rows = -(-positions * tiles // SELECT_ROWS) * SELECT_ROWS
    whole = pl.BlockSpec(source.shape, lambda i, *_: (0,) * source.ndim)
    return pl.pallas_call(
        kernel,
        out_shape=pltpu.HBM((4, tiles * tile_span), jnp.float32),
        grid_spec=pltpu.PrefetchScalarGridSpec(
            num_scalar_prefetch=3,
            grid=(tiles // sub,),
            in_specs=[whole, pl.BlockSpec((width, tile_span), lambda i, *_: (0, 0))],
            out_specs=pl.BlockSpec((4, sub * tile_span), lambda i, *_: (0, i)),
            scratch_shapes=[
                pltpu.VMEM((rows, tile_span), jnp.float32),
                pltpu.VMEM((positions, tiles, LANES), jnp.float32),
                *scratch,
            ],
        ),
    )(*scene, source, resample)


def slots_for(mean, owners, deviations):
    wanted = mean + deviations * mean**0.5
    capacity = min(LANES // 2, max(8, int(-(-wanted // 8) * 8)))
    while owners * capacity % (2 * LANES):
        capacity += 8
    return capacity


def on_device(cells, counts, donor_dest, donor_tile, depth_rank, resample, color_gain, color_bias):
    owners = lax.axis_size(AXES)
    group_count = lax.axis_size("grp")
    swap_count = lax.axis_size("swap")
    block_count, block_width = cells.shape
    tile_span = resample.shape[1]
    half_pixels = IMG_H // group_count * IMG_W
    layer_tiles = half_pixels // tile_span
    own_tiles = layer_tiles // swap_count
    positions = swap_count * DEPTH
    opacity_step = 2.5 / (DEPTH * swap_count)
    mean = block_count / owners
    capacities = (slots_for(mean, owners, 5.5), slots_for(mean * 4 / 7, owners, 5.0))
    band_width = block_width // BANDS
    plan = (owners, capacities, band_width, swap_count, layer_tiles, own_tiles)

    dest_row = donor_dest.reshape(1, block_count)
    tile_row = donor_tile.reshape(1, block_count)
    counts_row = counts.reshape(1, block_count)
    tag_row = band_width // LANES * sum(capacities) - (BANDS - 1) * capacities[-1] - 1

    def exchange(*turns):
        sent = pack(plan, turns, dest_row, tile_row, counts_row, cells)
        got = lax.all_to_all(sent, AXES, split_axis=0, concat_axis=0, tiled=True)
        return got, jnp.max(got[:, tag_row + (BANDS - 1) * capacities[-1]]) >= MORE

    def partial_sum(got):
        rows = jnp.arange(own_tiles * positions, dtype=jnp.int32)[:, None]
        top, sums = 0, []
        for band, capacity in enumerate(capacities):
            tags = got[:, tag_row + band * capacities[-1]].astype(jnp.int32)
            source = jnp.arange(owners)[:, None]
            slot = jnp.arange(capacity)[None, :]
            lane = source * capacity + slot
            tile = jnp.take_along_axis(tags, lane % LANES, axis=1)
            position = jnp.take_along_axis(tags, (lane + capacity) % LANES, axis=1)
            ids = (position ^ (depth_rank[0] * DEPTH)) * own_tiles + tile
            ids = jnp.where(slot < usable_slots(band, capacity), ids, -1).reshape(1, -1)
            selector = (ids == rows).astype(jnp.bfloat16)
            end = top + band_width // LANES * capacity
            data = got[:, top:end].reshape(owners, -1, capacity, LANES).transpose(0, 2, 1, 3)
            data = data.reshape(owners * capacity, band_width)
            sums.append(jnp.dot(selector, data, preferred_element_type=jnp.float32))
            top = end
        return jnp.concatenate(sums, axis=1)

    scene = (depth_rank, color_gain, color_bias)
    received, more = exchange()

    def one_round():
        kernel = functools.partial(gather_render_kernel, opacity_step, positions, capacities)
        slots = [owners * capacity for capacity in capacities]
        scratch = [pltpu.VMEM((count, band_width), jnp.bfloat16) for count in slots]
        scratch += [pltpu.VMEM((8, count), jnp.int32) for count in slots]
        scratch += [pltpu.VMEM((SELECT_ROWS, block_width), jnp.bfloat16)]
        scratch += [pltpu.SMEM((own_tiles // min(8, own_tiles) + 1,), jnp.int32)]
        return render(kernel, received, own_tiles, positions, scene, resample, scratch)

    def more_rounds():
        def next_round(state):
            turn, _, total = state
            got, again = exchange(turn.reshape(1))
            return turn + 1, again, total + partial_sum(got)

        start = (jnp.int32(1), more, partial_sum(received))
        total = lax.while_loop(lambda state: state[1], next_round, start)[2]
        kernel = functools.partial(render_kernel, opacity_step, positions)
        tile_cells = total.astype(jnp.bfloat16)
        return render(kernel, tile_cells, own_tiles, positions, scene, resample, [])

    return lax.cond(more, more_rounds, one_round)


def solution(mesh):
    placed = (
        P(("grp", "swap"), None),
        P(("grp", "swap")),
        P(("grp", "swap"), None),
        P(("grp", "swap")),
        P(),
        P(),
        P(),
        P(),
    )
    return jax.shard_map(
        on_device, mesh=mesh, in_specs=placed, out_specs=P(None, ("grp", "swap")), check_vma=False
    )
```

time: 71.7 us -> 68.6 us (0.957)
  blocking collectives: 0 us -> 47.8 us
  waiting for transfers between devices: 41.6 us -> 0 us
  starting transfers between devices: 7.34 us -> 0 us
  Pallas kernels: 21.1 us -> 20 us
    all_to_all x0 -> x1, blocking collectives: none -> 47.8 us  [exchange(): got = lax.all_to_all(sent, AXES, split_axis=0, concat_axis=0, tiled=True)]
    all_to_all x1 -> x0, waiting for transfers between devices: 41.6 us -> none  [exchange(): got = lax.all_to_all(sent, AXES, split_axis=0, concat_axis=0, tiled=True)]
    all_to_all x1 -> x0, starting transfers between devices: 7.34 us -> none  [exchange(): got = lax.all_to_all(sent, AXES, split_axis=0, concat_axis=0, tiled=True)]
    pallas_call x2, Pallas kernels: 21.1 us -> 20 us  [the longest x1 14.1 us: render(): pl.pallas_call(kernel, out_shape=pltpu.HBM((4, tiles * tile_span), jnp.fl...]
  transfers between devices with their start and end apart: 1 -> 0, of which waited for: 1 -> 0; matrix products, arithmetic and copies ran while one was open for 0% -> 0% of each run, Pallas kernels for 0% -> 0%
where the time goes in v4:
time: 68.6 us; the launch traced here: 69.1 us
  blocking collectives  47.8 us (70%)
  Pallas kernels  20 us (29%)
  between operations  0.7 us (1%)
    all_to_all x1, blocking collectives, exchange(): got = lax.all_to_all(sent, AXES, split_axis=0, concat_axis=0, tiled=True)  47.8 us
    pallas_call x1, Pallas kernels, render(): pl.pallas_call(kernel, out_shape=pltpu.HBM((4, tiles * tile_span), jnp.fl...  14.1 us
    pallas_call x1, Pallas kernels, pack(): pl.pallas_call(lambda *refs: pack_kernel(plan, refs[:len(turns)], *refs[l...  5.85 us

profile of v4, /device:TPU:0, one launch (start us, length us, event | category | flops | bytes accessed | tf_op | source)
XLA Modules:
  0.0 69.1 jit_solution(1181890646052478134)
XLA Ops:
  0.0 0.0 copy-start.15
  0.0 0.0 copy-start.12
  0.0 0.0 copy-start.3
  0.0 0.0 copy-start.9
  0.0 5.9 %shard_map.84 = bf16[32,208,128]{2,1,0:T(8,128)(2,1)} custom-call(s32[1,1024]{1,0:T(1,128)} %bitcast.112, s32[1,1024]{1,0:T(1,128)} %bitcast.114, s32[1,1024]{1,0:T(1,128)} %bitcast.116, bf16[1024,512]{1,0:T(8,128)(2,1)} %refs_3_.1), custom_call_target="tpu_custom_call" | custom-call | tf_op jit(solution)/shard_map/pallas_call | solution.py:168
  5.9 47.8 %all_to_all.14 = bf16[32,208,128]{2,1,0:T(8,128)(2,1)S(1)} all-to-all(bf16[32,208,128]{2,1,0:T(8,128)(2,1)} %shard_map.84), channel_id=1, replica_groups=mesh['grp'=2,'swap'=16] {'swap','grp'}, dimensions={0} | all-to-all | bytes 3407872 | tf_op jit(solution)/shard_map/all_to_all | solution.py:462
  53.7 0.6 slice_reduce_fusion.1
  55.0 0.0 copy-done.15
  55.0 0.0 copy-done.12
  55.0 0.0 copy-done.3
  55.0 0.0 copy-done.9
  55.0 14.1 %conditional.1 = (f32[4,32768]{1,0:T(4,128)}) conditional(s32[]{:T(128)} %convert_element_type.40, (s32[16]{0:T(128)S(1)}, f32[3]{0:T(128)S(1)}, f32[3]{0:T(128)S(1)}, bf16[32,208,128]{2,1,0:T(8,128)(2,1)S(1)}, bf16[512,1024]{1,0:T(8,128)(2,1)S(1)}) %tuple.71, (bf16[32,208,128]{2,1,0:T(8,128)(2,1)S(1)}, s32[16]{0:T(128)S(1)}, s32[1,1024]{1,0:T(1,128)}, ...), branch_computations={%region_1.0_spmd, %region_2.10_spmd} | conditional | flops 6996652544 | bytes 108137712 | solution.py:509
  55.0 14.1 %branch_0_fun.1 = f32[4,32768]{1,0:T(4,128)} custom-call(s32[16]{0:T(128)S(1)} %get-tuple-element.129.depth_rank, f32[3]{0:T(128)S(1)} %get-tuple-element.130.gain, f32[3]{0:T(128)S(1)} %get-tuple-element.131.bias, bf16[32,208,128]{2,1,0:T(8,128)(2,1)S(1)} %get-tuple-element.132.recv_ref, bf16[512,1024]{1,0:T(8,128)(2,1)S(1)} %get-tuple-element.133.resample_ref), custom_call_target="tpu_custom_call" | custom-call | tf_op jit(solution)/shard_map/cond/branch_0_fun/pallas_call | solution.py:414
Async XLA Ops:
  0.0 55.0 %copy-start.15 = (f32[3]{0:T(128)S(1)}, f32[3]{0:T(128)}, u32[]{:S(2)}) copy-start(f32[3]{0:T(128)} %param.27) | copy-start | bytes 40
  0.0 55.0 %copy-start.12 = (f32[3]{0:T(128)S(1)}, f32[3]{0:T(128)}, u32[]{:S(2)}) copy-start(f32[3]{0:T(128)} %param.26) | copy-start | bytes 40
  0.0 55.0 %copy-start.3 = (bf16[512,1024]{1,0:T(8,128)(2,1)S(1)}, bf16[512,1024]{1,0:T(8,128)(2,1)}, u32[]{:S(2)}) copy-start(bf16[512,1024]{1,0:T(8,128)(2,1)} %param.25) | copy-start | bytes 3145732
  0.0 55.0 %copy-start.9 = (s32[16]{0:T(128)S(1)}, s32[16]{0:T(128)}, u32[]{:S(2)}) copy-start(s32[16]{0:T(128)} %param.24) | copy-start | bytes 196

commit v5 on v4

--- a/solution.py
+++ b/solution.py
@@ -17,6 +17,7 @@
 AXES = ("swap", "grp")
 SELECT_ROWS = 384
 STEP_ROWS = 256
+INTEGRATE_LANES = 512
 BUCKET_STEP = 8
 LOG2_E = 1.4426950408889634
 EXP2_TOP = 126.0
@@ -70,7 +71,7 @@
         total = total + jnp.sum(part, axis=1, keepdims=True)
     before = jnp.concatenate(before, axis=1) * hits
 
-    lanes = lax.broadcasted_iota(jnp.int32, (LANES, block_count), 0)
+    lanes = lax.broadcasted_iota(jnp.int32, (LANES, block_count), 0).astype(jnp.int16)
     lane_of = lax.broadcasted_iota(jnp.int32, (1, LANES), 1)
     for band, capacity in enumerate(capacities):
         rows = slice(band * owners, (band + 1) * owners)
@@ -80,13 +81,16 @@
         alive = counts_ref[...] > band * band_width
         present = alive & (order >= 0) & (order < usable)
         slot_ref[band : band + 1, :] = jnp.where(present, target * capacity + order, -1)
-        placed = jnp.zeros((LANES, block_count), jnp.float32)
+        placed = jnp.zeros((LANES, block_count), jnp.bfloat16)
         for index, part in enumerate(parts):
             lane = (order + device * capacity + index * capacity) & (LANES - 1)
-            placed = jnp.where(lanes == jnp.where(present, lane, -1), part, placed)
+            lane = jnp.where(present, lane, -1).astype(jnp.int16)
+            same = lanes == jnp.broadcast_to(lane, lanes.shape)
+            part = jnp.broadcast_to(part.astype(jnp.bfloat16), lanes.shape)
+            placed = jnp.where(same, part, placed)
         tags = lax.dot_general(
             hits[rows].astype(jnp.bfloat16),
-            placed.astype(jnp.bfloat16),
+            placed,
             (((1,), (1,)), ((), ())),
             preferred_element_type=jnp.float32,
         )
@@ -102,11 +106,12 @@
 def mask_dead(counts_ref, cells_ref):
     block_count, width = cells_ref.shape
     live = jnp.transpose(jnp.broadcast_to(counts_ref[...], (LANES, block_count)))
-    lanes = lax.broadcasted_iota(jnp.int32, (block_count, LANES), 1)
+    live = live.astype(jnp.int16)
+    lanes = lax.broadcasted_iota(jnp.int32, (block_count, LANES), 1).astype(jnp.int16)
     for start in range(0, width, LANES):
         at = pl.ds(start, LANES)
-        keep = jnp.where(lanes + start < live, 1.0, 0.0).astype(jnp.bfloat16)
-        cells_ref[:, at] = cells_ref[:, at] * keep
+        alive = lanes + jnp.int16(start) < live
+        cells_ref[:, at] = jnp.where(alive, cells_ref[:, at], jnp.bfloat16(0))
 
 
 def pack_kernel(plan, turn_refs, dest_ref, tile_ref, counts_ref, cells_hbm, out_ref, *scratch):
@@ -189,37 +194,41 @@
     steps = STEP_ROWS // tiles
     half_gain = [0.5 * gain[k] for k in range(3)]
     half_bias = [0.5 * bias[k] for k in range(3)]
-
-    def block_step(block, state):
-        passing, fed, *colors = state
-        for inside in range(steps):
-            step = block * steps + inside
-            at = pl.multiple_of(step * tiles + group * sub, sub)
-            v = sample_ref[pl.ds(at, sub), :]
-            empty = empty_ref[step, pl.ds(pl.multiple_of(group * sub, sub), sub), :]
-            empty = jnp.concatenate([empty] * (span // LANES), axis=1)
-            scaled = v * LOG2_E
-            softplus = jnp.log2(1.0 + jnp.exp2(jnp.minimum(scaled, EXP2_TOP)))
-            softplus = jnp.maximum(scaled, softplus)
-            passed = passing * jnp.exp2(-opacity_step * softplus)
-            weight = (passing - passed) * empty
-            fed = fed + weight
-            for k in range(3):
-                colors[k] = colors[k] + weight * jnp.tanh(half_gain[k] * v + half_bias[k])
-            passing = passed
-        return (passing, fed, *colors)
-
-    zero = jnp.zeros((sub, span), jnp.float32)
-    passing, fed, *colors = lax.fori_loop(0, blocks, block_step, (zero + 1.0, zero) + (zero,) * 3)
     left = (positions - blocks * steps).astype(jnp.float32)
-    opacity = 1.0 - passing * jnp.exp2(zero - opacity_step * left)
-    rest = opacity - fed
-    planes = [
-        0.5 * (opacity + colors[k] + rest * jnp.tanh(zero + half_bias[k])) for k in range(3)
-    ] + [opacity]
-    for k, plane in enumerate(planes):
-        for row in range(sub):
-            out_ref[k : k + 1, row * span : (row + 1) * span] = plane[row : row + 1]
+    for start in range(0, span, INTEGRATE_LANES):
+        lanes = slice(start, start + INTEGRATE_LANES)
+
+        def block_step(block, state):
+            passing, fed, *colors = state
+            for inside in range(steps):
+                step = block * steps + inside
+                at = pl.multiple_of(step * tiles + group * sub, sub)
+                v = sample_ref[pl.ds(at, sub), lanes]
+                empty = empty_ref[step, pl.ds(pl.multiple_of(group * sub, sub), sub), :]
+                empty = jnp.concatenate([empty] * (INTEGRATE_LANES // LANES), axis=1)
+                scaled = v * LOG2_E
+                softplus = jnp.log2(1.0 + jnp.exp2(jnp.minimum(scaled, EXP2_TOP)))
+                softplus = jnp.maximum(scaled, softplus)
+                passed = passing * jnp.exp2(-opacity_step * softplus)
+                weight = (passing - passed) * empty
+                fed = fed + weight
+                for k in range(3):
+                    colors[k] = colors[k] + weight * jnp.tanh(half_gain[k] * v + half_bias[k])
+                passing = passed
+            return (passing, fed, *colors)
+
+        zero = jnp.zeros((sub, INTEGRATE_LANES), jnp.float32)
+        state = (zero + 1.0, zero) + (zero,) * 3
+        passing, fed, *colors = lax.fori_loop(0, blocks, block_step, state)
+        opacity = 1.0 - passing * jnp.exp2(zero - opacity_step * left)
+        rest = opacity - fed
+        planes = [
+            0.5 * (opacity + colors[k] + rest * jnp.tanh(zero + half_bias[k])) for k in range(3)
+        ] + [opacity]
+        for k, plane in enumerate(planes):
+            for row in range(sub):
+                at = row * span + start
+                out_ref[k : k + 1, at : at + INTEGRATE_LANES] = plane[row : row + 1]
 
 
 def render_kernel(
@@ -506,7 +515,8 @@
         tile_cells = total.astype(jnp.bfloat16)
         return render(kernel, tile_cells, own_tiles, positions, scene, resample, [])
 
-    return lax.cond(more, more_rounds, one_round)
+    frame = one_round()
+    return lax.cond(more, more_rounds, lambda: frame)
 
 
 def solution(mesh):

time: 68.6 us -> 67.4 us (0.983); the launches traced: 69.1 us -> 67 us
  Pallas kernels: 20 us -> 17.9 us
    pallas_call x1, Pallas kernels: 14.1 us -> 12.2 us  [render(): pl.pallas_call(kernel, out_shape=pltpu.HBM((4, tiles * tile_span), jnp.fl...]
where the time goes in v5:
time: 67.4 us; the launch traced here: 67 us
  blocking collectives  47.8 us (71%)
  Pallas kernels  17.9 us (27%)
  between operations  0.7 us (1%)
    all_to_all x1, blocking collectives, exchange(): got = lax.all_to_all(sent, AXES, split_axis=0, concat_axis=0, tiled=True)  47.8 us
    pallas_call x1, Pallas kernels, render(): pl.pallas_call(kernel, out_shape=pltpu.HBM((4, tiles * tile_span), jnp.fl...  12.2 us
    pallas_call x1, Pallas kernels, pack(): pl.pallas_call(lambda *refs: pack_kernel(plan, refs[:len(turns)], *refs[l...  5.72 us

profile of v5, /device:TPU:0, one launch (start us, length us, event | category | flops | bytes accessed | tf_op | source)
XLA Modules:
  0.0 67.0 jit_solution(13059738447183935527)
XLA Ops:
  0.0 0.0 copy-start.13
  0.0 0.0 copy-start.11
  0.0 0.0 copy-start.3
  0.0 0.0 copy-start.8
  0.0 5.7 %shard_map.84 = bf16[32,208,128]{2,1,0:T(8,128)(2,1)} custom-call(s32[1,1024]{1,0:T(1,128)} %bitcast.112, s32[1,1024]{1,0:T(1,128)} %bitcast.114, s32[1,1024]{1,0:T(1,128)} %bitcast.116, bf16[1024,512]{1,0:T(8,128)(2,1)} %refs_3_.1), custom_call_target="tpu_custom_call" | custom-call | tf_op jit(solution)/shard_map/pallas_call | solution.py:173
  5.7 47.8 %all_to_all.14.recv_ref = bf16[32,208,128]{2,1,0:T(8,128)(2,1)S(1)} all-to-all(bf16[32,208,128]{2,1,0:T(8,128)(2,1)} %shard_map.84), channel_id=1, replica_groups=mesh['grp'=2,'swap'=16] {'swap','grp'}, dimensions={0} | all-to-all | bytes 3407872 | tf_op jit(solution)/shard_map/all_to_all | solution.py:471
  53.5 0.6 slice_reduce_fusion.1
  54.8 0.0 copy-done.13
  54.8 0.0 copy-done.11
  54.9 0.0 copy-done.3
  54.9 0.0 copy-done.8
  54.9 12.2 %shard_map.85 = f32[4,32768]{1,0:T(4,128)} custom-call(s32[16]{0:T(128)S(1)} %copy-done.8, f32[3]{0:T(128)S(1)} %copy-done.11, f32[3]{0:T(128)S(1)} %copy-done.13, bf16[32,208,128]{2,1,0:T(8,128)(2,1)S(1)} %all_to_all.14.recv_ref, bf16[512,1024]{1,0:T(8,128)(2,1)S(1)} %copy-done.3), custom_call_target="tpu_custom_call" | custom-call | tf_op jit(solution)/shard_map/pallas_call | solution.py:423
  (1 shorter events, 0.0 us)
Async XLA Ops:
  0.0 54.8 %copy-start.13 = (f32[3]{0:T(128)S(1)}, f32[3]{0:T(128)}, u32[]{:S(2)}) copy-start(f32[3]{0:T(128)} %bias.1) | copy-start | bytes 40
  0.0 54.8 %copy-start.11 = (f32[3]{0:T(128)S(1)}, f32[3]{0:T(128)}, u32[]{:S(2)}) copy-start(f32[3]{0:T(128)} %gain.1) | copy-start | bytes 40
  0.0 54.9 %copy-start.3 = (bf16[512,1024]{1,0:T(8,128)(2,1)S(1)}, bf16[512,1024]{1,0:T(8,128)(2,1)}, u32[]{:S(2)}) copy-start(bf16[512,1024]{1,0:T(8,128)(2,1)} %resample_ref.1) | copy-start | bytes 3145732
  0.0 54.9 %copy-start.8 = (s32[16]{0:T(128)S(1)}, s32[16]{0:T(128)}, u32[]{:S(2)}) copy-start(s32[16]{0:T(128)} %depth_rank.1) | copy-start | bytes 196
